TPU v7x, 128 devices: a whole 4x4x4 slice. The times are simulated.
128 devices in a mesh: dp: 4 (over z), fsdp: 32 (over x, y, core).
Axes of the slice: x: 4, y: 4, z: 4, core: 2. Of those that a mesh axis runs over, the one named last changes fastest.
Arguments:
- tokens: bfloat16 [32768, 6144], P(('dp', 'fsdp')), may hold values from -6 to 6
- cotangent: bfloat16 [32768, 6144], P(('dp', 'fsdp')), may hold values from -6 to 6
- up_weight_blocks: bfloat16 [128, 128, 128], P('fsdp'), may hold values from -0.5 to 0.5
- down_weight_blocks: bfloat16 [128, 128, 128], P('fsdp'), may hold values from -0.5 to 0.5
- block_rows: int32 [128], replicated, may hold values from 0 to 47, as said below
- block_cols: int32 [128], replicated, may hold values from 0 to 191
- owner_counts: int32 [32], replicated, may hold values from 1 to 4, as said below
Outputs:
- output: bfloat16 [32768, 6144], P(('dp', 'fsdp'))
- input_grad: bfloat16 [32768, 6144], P(('dp', 'fsdp'))
- up_grad: float32 [128, 128, 128], P('fsdp')
- down_grad: float32 [128, 128, 128], P('fsdp')
Inputs may be any that keep to these rules, and one draw needn't show every extreme that they name: Owner o has owner_counts[o] live slots, its first ones; some owner has all 4 live. All 128 slots name distinct (block_rows, block_cols) pairs.
All inputs are finite; a program needn't handle non-finite values.
Results may differ from a plain program's by a relative error of at most 0.0049.
Values may be sent and summed in bfloat16 or wider, within the bound.
A program may use at most 256 MiB of HBM per device.

v0:
```python
import math

import jax
import jax.numpy as jnp
from jax import lax
from jax.sharding import PartitionSpec as P

D = 6144
FF = 24576
BLOCK_EDGE = 128
SLOTS = 4


gelu_scale = 0.7978845608028654
cubic_coef = 0.044715


def gelu_parts(values):
    inner_arg = gelu_scale * (values + cubic_coef * values * values * values)
    tanh_val = jnp.tanh(inner_arg)
    gelu_value = 0.5 * values * (1.0 + tanh_val)
    gelu_slope = 0.5 * (1.0 + tanh_val) + 0.5 * values * (
        1.0 - tanh_val * tanh_val
    ) * gelu_scale * (1.0 + 3.0 * cubic_coef * values * values)
    return (gelu_value, gelu_slope)


def to_blocks(source):
    token_count = source.shape[0]
    return source.reshape(token_count, source.shape[1] // BLOCK_EDGE, BLOCK_EDGE).transpose(1, 0, 2)


def from_blocks(blocks):
    return blocks.transpose(1, 0, 2).reshape(blocks.shape[1], blocks.shape[0] * BLOCK_EDGE)


def one_hot_table(index_list, width, dtype):
    return (index_list[:, None] == jnp.arange(width, dtype=jnp.int32)[None, :]).astype(dtype)


def pick_blocks(blocks, index_list):
    table = one_hot_table(index_list, blocks.shape[0], jnp.bfloat16)
    return jnp.einsum("sr,rnk->snk", table, blocks, preferred_element_type=jnp.float32).astype(
        jnp.bfloat16
    )


def spread_blocks(contrib, index_list, width):
    table = one_hot_table(index_list, width, jnp.float32)
    return jnp.einsum(
        "sc,snj->cnj",
        table,
        contrib,
        preferred_element_type=jnp.float32,
        precision=lax.Precision.HIGHEST,
    )


def on_device(
    tokens, cotangent, up_weight_blocks, down_weight_blocks, block_rows, block_cols, owner_counts
):
    token_count = tokens.shape[0]
    total_slots = block_rows.shape[0]
    row_blocks = D // BLOCK_EDGE
    col_blocks = FF // BLOCK_EDGE
    slot_position = jnp.arange(total_slots, dtype=jnp.int32)
    live_mask = slot_position % SLOTS < owner_counts[slot_position // SLOTS]
    x_blocks = to_blocks(tokens)
    dy_blocks = to_blocks(cotangent)

    def slot_info():
        return (block_rows, block_cols, live_mask.astype(jnp.bfloat16)[:, None, None])

    up_whole = lax.all_gather(up_weight_blocks, "fsdp", axis=0, tiled=True)
    row_ids, col_ids, keep_mask = slot_info()
    picked = pick_blocks(x_blocks, row_ids)
    contrib = jnp.einsum(
        "snk,skj->snj", picked, up_whole * keep_mask, preferred_element_type=jnp.float32
    )
    pre_act = spread_blocks(contrib, col_ids, col_blocks)
    gelu_value, gelu_slope = gelu_parts(pre_act)
    hidden = gelu_value.astype(jnp.bfloat16)
    row_ids, col_ids, keep_mask = slot_info()
    weights = lax.all_gather(down_weight_blocks, "fsdp", axis=0, tiled=True) * keep_mask
    h_pick = pick_blocks(hidden, col_ids)
    dy_pick = pick_blocks(dy_blocks, row_ids)
    out_part = jnp.einsum("snk,skj->snj", h_pick, weights, preferred_element_type=jnp.float32)
    back_part = jnp.einsum("snj,skj->snk", dy_pick, weights, preferred_element_type=jnp.float32)
    out_sum = spread_blocks(out_part, row_ids, row_blocks)
    hidden_grad = spread_blocks(back_part, col_ids, col_blocks)
    output = from_blocks(out_sum.astype(jnp.bfloat16))
    pre_grad = (hidden_grad * gelu_slope).astype(jnp.bfloat16)
    row_ids, col_ids, keep_mask = slot_info()
    picked = pick_blocks(pre_grad, col_ids)
    contrib = jnp.einsum(
        "snj,skj->snk", picked, up_whole * keep_mask, preferred_element_type=jnp.float32
    )
    in_sum = spread_blocks(contrib, row_ids, row_blocks)
    input_grad = from_blocks(in_sum.astype(jnp.bfloat16))
    dp_groups = lax.axis_size("dp")
    fsdp_owners = lax.axis_size("fsdp")
    grad_scale = 1.0 / math.sqrt(token_count * dp_groups * fsdp_owners)
    slot_list = jnp.arange(lax.axis_size("fsdp") * SLOTS, dtype=jnp.int32)
    keep_mask = live_mask[slot_list].astype(jnp.float32)[:, None, None]
    x_pick = pick_blocks(x_blocks, block_rows[slot_list])
    p_pick = pick_blocks(pre_grad, block_cols[slot_list])
    up_local = lax.psum_scatter(
        jnp.einsum("snk,snj->skj", x_pick, p_pick, preferred_element_type=jnp.float32) * keep_mask,
        "fsdp",
        scatter_dimension=0,
        tiled=True,
    )
    slot_list = jnp.arange(lax.axis_size("fsdp") * SLOTS, dtype=jnp.int32)
    keep_mask = live_mask[slot_list].astype(jnp.float32)[:, None, None]
    h_pick = pick_blocks(hidden, block_cols[slot_list])
    dy_pick = pick_blocks(dy_blocks, block_rows[slot_list])
    down_local = lax.psum_scatter(
        jnp.einsum("snk,snj->skj", h_pick, dy_pick, preferred_element_type=jnp.float32) * keep_mask,
        "fsdp",
        scatter_dimension=0,
        tiled=True,
    )
    up_grad, down_grad = lax.psum((up_local, down_local), "dp")
    return (output, input_grad, up_grad * grad_scale, down_grad * grad_scale)


def solution(mesh):
    in_specs = (
        P(("dp", "fsdp"), None),
        P(("dp", "fsdp"), None),
        P("fsdp", None, None),
        P("fsdp", None, None),
        P(),
        P(),
        P(),
    )
    out_specs = (
        P(("dp", "fsdp"), None),
        P(("dp", "fsdp"), None),
        P("fsdp", None, None),
        P("fsdp", None, None),
    )
    return jax.shard_map(
        on_device, mesh=mesh, in_specs=in_specs, out_specs=out_specs, check_vma=False
    )
```

profile of v0, /device:TPU:1, one launch (start us, length us, event | category | flops | bytes accessed | tf_op | source)
XLA Modules:
  0.0 444.7 jit_solution(9239581407377566130)
XLA Ops:
  7.2 0.0 copy-start
  7.2 0.0 copy-start.4
  7.2 0.0 copy-start.2
  7.2 0.0 all-gather.3.cloned.1.call-start
  7.2 0.7 all-gather.3.cloned.1.call-update
  7.9 0.0 all-gather.5.cloned.1.call-start
  8.0 0.7 all-gather.5.cloned.1.call-update
  8.7 0.0 reduce-scatter.3.cloned.1.call-start
  8.7 0.0 copy-start.7
  8.7 4.4 copy.23
  13.2 0.0 copy-done.7
  13.2 0.7 copy.25
  13.9 0.0 copy-done.4
  13.9 1.2 gather_fusion.2
  15.2 1.2 gather_fusion.1
  16.5 1.2 gather_fusion
  17.7 1.4 gather_fusion.3
  19.1 7.5 %convolution_convert_fusion.7 = bf16[128,256,128]{2,0,1:T(8,128)(2,1)} fusion(bf16[256,48,128]{2,1,0:T(8,128)(2,1)} %bitcast.50, s32[128]{0:T(128)S(1)} %copy-done.2), kind=kOutput, calls=%fused_computation.43 | convolution fusion | flops 406853632 | bytes 11534848 | tf_op jit(solution)/shard_map/sr,rnk->snk/dot_general | solution.py:43
  26.6 5.6 %convolution_convert_fusion.5 = bf16[128,256,128]{2,0,1:T(8,128)(2,1)} fusion(bf16[256,48,128]{2,1,0:T(8,128)(2,1)S(1)} %bitcast.48, s32[128]{0:T(128)S(1)} %copy-done.2), kind=kOutput, calls=%fused_computation.41 | convolution fusion | flops 406853632 | bytes 11534848 | tf_op jit(solution)/shard_map/sr,rnk->snk/dot_general | solution.py:43
  32.2 5.6 %convolution_convert_fusion.3 = bf16[128,256,128]{2,0,1:T(8,128)(2,1)} fusion(bf16[256,48,128]{2,1,0:T(8,128)(2,1)S(1)} %bitcast.51, s32[128]{0:T(128)S(1)} %gather_fusion.1), kind=kOutput, calls=%fused_computation.39 | convolution fusion | flops 406853632 | bytes 11534848 | tf_op jit(solution)/shard_map/sr,rnk->snk/dot_general | solution.py:43
  37.9 22.1 %all-gather.3.cloned.1.call-done = bf16[128,128,128]{2,1,0:T(8,128)(2,1)} async-done(((bf16[4,128,128]{2,1,0:T(8,128)(2,1)}), bf16[128,128,128]{2,1,0:T(8,128)(2,1)}) %all-gather.3.cloned.1.call-update) | async-done | bytes 4194320 | tf_op jit(solution)/shard_map/all_gather | solution.py:74
  59.9 18.8 %fusion.27 = f32[128,256,128]{2,1,0:T(8,128)} fusion(bf16[128,256,128]{2,0,1:T(8,128)(2,1)} %convolution_convert_fusion.7, bf16[128,128,128]{2,1,0:T(8,128)(2,1)} %all-gather.3.cloned.1.call-done, bf16[128]{0:T(256)(128)(2,1)S(1)} %get-tuple-element.6), kind=kOutput, calls=%fused_computation.34 | convolution fusion | flops 1075838976 | bytes 29360384 | tf_op jit(solution)/shard_map/snk,skj->snj/dot_general | solution.py:77
  78.7 30.3 %fusion.13 = f32[192,256,128]{2,0,1:T(8,128)} fusion(f32[128,256,128]{2,1,0:T(8,128)} %fusion.27, s32[128]{0:T(128)S(1)} %copy-done.4), kind=kOutput, calls=%fused_computation.20 | convolution fusion | flops 9663700992 | bytes 41943552 | tf_op jit(solution)/shard_map/sc,snj->cnj/dot_general | solution.py:50
  109.1 0.0 all-gather.5.cloned.1.call-done
  109.1 18.5 %fusion.23 = f32[128,256,128]{2,1,0:T(8,128)} fusion(bf16[128,256,128]{2,0,1:T(8,128)(2,1)} %convolution_convert_fusion.5, bf16[128,128,128]{2,1,0:T(8,128)(2,1)} %all-gather.5.cloned.1.call-done, bf16[128]{0:T(256)(128)(2,1)S(1)} %get-tuple-element.6), kind=kOutput, calls=%fused_computation.30 | convolution fusion | flops 1075838976 | bytes 29360384 | tf_op jit(solution)/shard_map/snj,skj->snk/dot_general | solution.py:88
  127.7 44.2 %fusion.6 = bf16[192,256,128]{2,0,1:T(8,128)(2,1)S(1)} fusion(f32[192,256,128]{2,0,1:T(8,128)} %fusion.13, f32[128,256,128]{2,1,0:T(8,128)} %fusion.23, s32[128]{0:T(128)S(1)} %copy-done.4), kind=kOutput, calls=%fused_computation.12 | convolution fusion | flops 9783238656 | bytes 54526464 | tf_op jit(solution)/shard_map/sc,snj->cnj/dot_general | solution.py:50
  171.9 4.6 %copy-done.5 = bf16[192,256,128]{2,0,1:T(8,128)(2,1)} copy-done((bf16[192,256,128]{2,0,1:T(8,128)(2,1)}, bf16[192,256,128]{2,0,1:T(8,128)(2,1)S(1)}, u32[]{:S(2)}) %copy-start.5) | copy-done | bytes 12582936
  176.5 5.6 %convolution_convert_fusion.2 = bf16[128,256,128]{2,0,1:T(8,128)(2,1)} fusion(bf16[192,256,128]{2,0,1:T(8,128)(2,1)S(1)} %fusion.6, s32[128]{0:T(128)S(1)} %gather_fusion.2), kind=kOutput, calls=%fused_computation.38 | convolution fusion | flops 1614831616 | bytes 20972032 | tf_op jit(solution)/shard_map/sr,rnk->snk/dot_general | solution.py:43
  182.1 23.2 %broadcast_multiply_fusion.1 = f32[128,128,128]{2,1,0:T(8,128)} fusion(f32[128]{0:T(128)S(1)} %convert_element_type.86, bf16[128,256,128]{2,0,1:T(8,128)(2,1)} %convolution_convert_fusion.2, bf16[128,256,128]{2,0,1:T(8,128)(2,1)} %convolution_convert_fusion.3), kind=kOutput, calls=%fused_computation.45 | convolution fusion | flops 1075838976 | bytes 25166336 | tf_op jit(solution)/shard_map/snk,snj->skj/dot_general | solution.py:108
  205.3 0.0 reduce-scatter.3.cloned.1.call-update
  205.3 0.0 reduce-scatter.5.cloned.1.call-start
  205.3 5.6 %convolution_convert_fusion = bf16[128,256,128]{2,0,1:T(8,128)(2,1)} fusion(bf16[256,48,128]{2,1,0:T(8,128)(2,1)S(1)} %bitcast.49, s32[128]{0:T(128)S(1)} %gather_fusion.1), kind=kOutput, calls=%fused_computation.36 | convolution fusion | flops 406853632 | bytes 11534848 | tf_op jit(solution)/shard_map/sr,rnk->snk/dot_general | solution.py:43
  211.0 17.0 %convolution_convert_fusion.1 = bf16[128,256,128]{2,0,1:T(8,128)(2,1)} fusion(s32[128]{0:T(128)S(1)} %gather_fusion.2, f32[192,256,128]{2,0,1:T(8,128)} %fusion.13), kind=kOutput, calls=%fused_computation.37 | convolution fusion | flops 1671454720 | bytes 33554944 | tf_op jit(solution)/shard_map/sr,rnk->snk/dot_general | solution.py:43
  228.0 23.8 %broadcast_multiply_fusion = f32[128,128,128]{2,1,0:T(8,128)} fusion(f32[128]{0:T(128)S(1)} %convert_element_type.86, bf16[128,256,128]{2,0,1:T(8,128)(2,1)} %convolution_convert_fusion, bf16[128,256,128]{2,0,1:T(8,128)(2,1)} %convolution_convert_fusion.1), kind=kOutput, calls=%fused_computation.44 | convolution fusion | flops 1075838976 | bytes 25166336 | tf_op jit(solution)/shard_map/snk,snj->skj/dot_general | solution.py:118
  251.8 0.0 reduce-scatter.5.cloned.1.call-update
  251.9 0.0 all-reduce.3.cloned.1.call-start
  251.9 11.0 %convolution_convert_fusion.4 = bf16[128,256,128]{2,0,1:T(8,128)(2,1)} fusion(bf16[192,256,128]{2,0,1:T(8,128)(2,1)} %copy-done.5, s32[128]{0:T(128)S(1)} %copy-done.4), kind=kOutput, calls=%fused_computation.40 | convolution fusion | flops 1614831616 | bytes 20972032 | tf_op jit(solution)/shard_map/sr,rnk->snk/dot_general | solution.py:43
  262.9 18.9 %fusion.21 = f32[128,256,128]{2,1,0:T(8,128)} fusion(bf16[128,256,128]{2,0,1:T(8,128)(2,1)} %convolution_convert_fusion.4, bf16[128,128,128]{2,1,0:T(8,128)(2,1)} %all-gather.3.cloned.1.call-done, bf16[128]{0:T(256)(128)(2,1)S(1)} %get-tuple-element.6), kind=kOutput, calls=%fused_computation.28 | convolution fusion | flops 1075838976 | bytes 29360384 | tf_op jit(solution)/shard_map/snj,skj->snk/dot_general | solution.py:95
  281.8 21.6 %fusion.48 = bf16[48,256,128]{2,0,1:T(8,128)(2,1)S(1)} fusion(f32[128,256,128]{2,1,0:T(8,128)} %fusion.21, s32[128]{0:T(128)S(1)} %copy-done.3), kind=kOutput, calls=%fused_computation.57 | convolution fusion | flops 2417498112 | bytes 19923456 | tf_op jit(solution)/shard_map/sc,snj->cnj/dot_general | solution.py:50
  303.4 16.6 %convolution_convert_fusion.6 = bf16[128,256,128]{2,0,1:T(8,128)(2,1)} fusion(s32[128]{0:T(128)S(1)} %copy-done.4, f32[192,256,128]{2,0,1:T(8,128)} %fusion.13), kind=kOutput, calls=%fused_computation.42 | convolution fusion | flops 1671454720 | bytes 33554944 | tf_op jit(solution)/shard_map/sr,rnk->snk/dot_general | solution.py:43
  320.1 19.8 %fusion.25 = f32[128,256,128]{2,1,0:T(8,128)} fusion(bf16[128,256,128]{2,0,1:T(8,128)(2,1)} %convolution_convert_fusion.6, bf16[128,128,128]{2,1,0:T(8,128)(2,1)} %all-gather.5.cloned.1.call-done, bf16[128]{0:T(256)(128)(2,1)S(1)} %get-tuple-element.6), kind=kOutput, calls=%fused_computation.32 | convolution fusion | flops 1075838976 | bytes 29360384 | tf_op jit(solution)/shard_map/snk,skj->snj/dot_general | solution.py:87
  339.9 22.4 %fusion.45 = bf16[48,256,128]{2,0,1:T(8,128)(2,1)} fusion(f32[128,256,128]{2,1,0:T(8,128)} %fusion.25, s32[128]{0:T(128)S(1)} %copy-done.3), kind=kOutput, calls=%fused_computation.56 | convolution fusion | flops 2417498112 | bytes 19923456 | tf_op jit(solution)/shard_map/sc,snj->cnj/dot_general | solution.py:50
  362.3 29.1 %reduce-scatter.5.cloned.1.call-done = f32[4,128,128]{2,1,0:T(8,128)} async-done(((f32[128,128,128]{2,1,0:T(8,128)}), f32[4,128,128]{2,1,0:T(8,128)}) %reduce-scatter.5.cloned.1.call-update) | async-done | bytes 262160 | tf_op jit(solution)/shard_map/reduce_scatter | solution.py:117
  391.4 0.0 all-reduce.3.cloned.1.call-update
  391.4 6.1 %copy_bitcast_fusion = (bf16[256,6144]{1,0:T(8,128)(2,1)}, bf16[256,6144]{1,0:T(8,128)(2,1)}) fusion(bf16[32,8,48,128]{3,2,1,0:T(8,128)(2,1)S(1)} %bitcast.52, bf16[32,8,48,128]{3,2,1,0:T(8,128)(2,1)} %bitcast.53), kind=kLoop, calls=%fused_computation.50 | loop fusion | bytes 12582912 | tf_op jit(solution)/shard_map/reshape | solution.py:34
  397.5 38.6 %all-reduce.3.cloned.1.call-done = (f32[4,128,128]{2,1,0:T(8,128)}, f32[4,128,128]{2,1,0:T(8,128)}) async-done(((f32[4,128,128]{2,1,0:T(8,128)}, f32[4,128,128]{2,1,0:T(8,128)}), (f32[4,128,128]{2,1,0:T(8,128)}, f32[4,128,128]{2,1,0:T(8,128)})) %all-reduce.3.cloned.1.call-update) | async-done | bytes 524304 | tf_op jit(solution)/shard_map/psum | solution.py:123
  436.1 1.9 broadcast_multiply_fusion.2
  437.9 0.0 copy-done.1
  (15 shorter events, 0.1 us)
Async XLA Ops:
  7.2 9.3 %copy-start = (s32[32]{0:T(128)S(1)}, s32[32]{0:T(128)}, u32[]{:S(2)}) copy-start(s32[32]{0:T(128)} %param.13) | copy-start | bytes 388
  7.2 6.8 %copy-start.4 = (s32[128]{0:T(128)S(1)}, s32[128]{0:T(128)}, u32[]{:S(2)}) copy-start(s32[128]{0:T(128)} %param.12) | copy-start | bytes 1540
  7.2 8.0 %copy-start.2 = (s32[128]{0:T(128)S(1)}, s32[128]{0:T(128)}, u32[]{:S(2)}) copy-start(s32[128]{0:T(128)} %param.11) | copy-start | bytes 1540
  7.2 52.7 %all-gather.3.cloned.1.call-start = ((), (), s32[]{:S(2)}) async-start(), calls=%async_computation.2 | async-start | bytes 4325376 | tf_op jit(solution)/shard_map/all_gather | solution.py:74
  7.9 101.2 %all-gather.5.cloned.1.call-start = ((), (), s32[]{:S(2)}) async-start(), calls=%async_computation.3 | async-start | bytes 4325376 | tf_op jit(solution)/shard_map/all_gather | solution.py:84
  8.7 353.6 %reduce-scatter.3.cloned.1.call-start = ((), (), s32[]{:S(2)}) async-start(), calls=%async_computation.4 | async-start | bytes 8650752 | tf_op jit(solution)/shard_map/reduce_scatter | solution.py:107
  8.7 4.4 copy-start.7
  26.6 5.6 %copy-start.6 = (bf16[32,8,48,128]{3,2,1,0:T(8,128)(2,1)S(1)}, bf16[32,8,48,128]{3,2,1,0:T(8,128)(2,1)}, u32[]{:S(2)}) copy-start(bf16[32,8,48,128]{3,2,1,0:T(8,128)(2,1)} %copy.23) | copy-start | bytes 9437188
  171.9 4.6 %copy-start.5 = (bf16[192,256,128]{2,0,1:T(8,128)(2,1)}, bf16[192,256,128]{2,0,1:T(8,128)(2,1)S(1)}, u32[]{:S(2)}) copy-start(bf16[192,256,128]{2,0,1:T(8,128)(2,1)S(1)} %fusion.6) | copy-start | bytes 37748740
  205.3 186.1 %reduce-scatter.5.cloned.1.call-start = ((), (), s32[]{:S(2)}) async-start(), calls=%async_computation.5 | async-start | bytes 8650752 | tf_op jit(solution)/shard_map/reduce_scatter | solution.py:117
  251.9 184.2 %all-reduce.3.cloned.1.call-start = ((), (), s32[]{:S(2)}) async-start(), calls=%async_computation.6 | async-start | bytes 1048576 | tf_op jit(solution)/shard_map/psum | solution.py:123
  262.9 18.9 %copy-start.3 = (s32[128]{0:T(128)S(1)}, s32[128]{0:T(128)}, u32[]{:S(2)}) copy-start(s32[128]{0:T(128)} %param.11) | copy-start | bytes 1540
  339.9 98.0 %copy-start.1 = (s32[32]{0:T(128)S(1)}, s32[32]{0:T(128)}, u32[]{:S(2)}) copy-start(s32[32]{0:T(128)} %param.13) | copy-start | bytes 388
Sparse Core Ops, SparseCore 0:
  10.3 49.5 all-gather.2
  62.2 45.3 all-gather.4
  205.4 89.8 reduce-scatter.2
  299.4 91.9 reduce-scatter.4
  393.6 42.4 all-reduce.2
where the time goes:
time: 449 us; the launch traced here: 445 us
  matrix products  316 us (70%)
  waiting for transfers between devices  91.2 us (20%)
  local copies, waits for them, and re-layouts  21 us (5%)
  between operations  14.2 us (3%)
    dot_general x4, matrix products, spread_blocks(): jnp.einsum('sc,snj->cnj', table, contrib, preferred_element_type=jnp.floa...  119 us
    dot_general x8, matrix products, pick_blocks(): jnp.einsum('sr,rnk->snk', table, blocks, preferred_element_type=jnp.float32)  74.6 us
    psum x1, waiting for transfers between devices, on_device(): up_grad, down_grad = lax.psum((up_local, down_local), 'dp')  38.6 us
    reduce_scatter x1, waiting for transfers between devices, on_device(): lax.psum_scatter(jnp.einsum('snk,snj->skj', h_pick, dy_pick, preferred_el...  29.1 us
    dot_general x1, matrix products, on_device(): jnp.einsum('snk,snj->skj', h_pick, dy_pick, preferred_element_type=jnp.fl...  23.8 us
    dot_general x1, matrix products, on_device(): jnp.einsum('snk,snj->skj', x_pick, p_pick, preferred_element_type=jnp.flo...  23.2 us
    all_gather x1, waiting for transfers between devices, on_device(): up_whole = lax.all_gather(up_weight_blocks, 'fsdp', axis=0, tiled=True)  22.1 us
    dot_general x1, matrix products, on_device(): jnp.einsum('snk,skj->snj', h_pick, weights, preferred_element_type=jnp.fl...  19.8 us
  transfers between devices with their start and end apart: 5, of which 3 were waited for; matrix products, arithmetic and copies ran while one was open for 54% of the time, Pallas kernels for 0%

commit v1 on v0

v1 whole, which is shorter than its diff:
```python
import functools
import math

import jax
import jax.numpy as jnp
from jax import lax
from jax.experimental import pallas as pl
from jax.experimental.pallas import tpu as pltpu
from jax.sharding import PartitionSpec as P

EDGE = 128
SLOTS = 4
RING = 4
MESH_ID = pl.DeviceIdType.MESH
BF16 = jnp.bfloat16
F32 = jnp.float32

gelu_scale = 0.7978845608028654
cubic_coef = 0.044715


def gelu_parts(values):
    inner_arg = gelu_scale * (values + cubic_coef * values * values * values)
    tanh_val = jnp.tanh(inner_arg)
    gelu_value = 0.5 * values * (1.0 + tanh_val)
    gelu_slope = 0.5 * (1.0 + tanh_val) + 0.5 * values * (
        1.0 - tanh_val * tanh_val
    ) * gelu_scale * (1.0 + 3.0 * cubic_coef * values * values)
    return gelu_value, gelu_slope


class Spot:
    def __init__(self):
        me = lax.axis_index("fsdp")
        self.z = lax.axis_index("dp")
        self.c = lax.rem(me, 2)
        self.y = lax.rem(me // 2, RING)
        self.x = me // (2 * RING)

    def owner(self, i, j, c=None):
        c = self.c if c is None else c
        x = lax.rem(self.x + i * (1 - c) + j * c, RING)
        y = lax.rem(self.y + i * c + j * (1 - c), RING)
        return (x * RING + y) * 2 + c

    def sibling(self):
        return (self.x * RING + self.y) * 2 + (1 - self.c)


def greet(targets):
    barrier = pltpu.get_barrier_semaphore()
    for target in targets:
        pl.semaphore_signal(barrier, inc=1, device_id=target, device_id_type=MESH_ID)
    pl.semaphore_wait(barrier, len(targets))


class Mail:
    def __init__(self, send_sem, recv_sem):
        self.send_sem, self.recv_sem = send_sem, recv_sem
        self.keys, self.sent = {}, []

    def slot(self, key):
        return self.keys.setdefault(key, len(self.keys))

    def send(self, src, dst, target, key):
        copy = pltpu.make_async_remote_copy(
            src_ref=src,
            dst_ref=dst,
            send_sem=self.send_sem.at[len(self.sent)],
            recv_sem=self.recv_sem.at[self.slot(key)],
            device_id=target,
            device_id_type=MESH_ID,
        )
        copy.start()
        self.sent.append(copy)

    def wait(self, dst, key, target):
        pltpu.make_async_remote_copy(
            src_ref=dst,
            dst_ref=dst,
            send_sem=self.send_sem.at[0],
            recv_sem=self.recv_sem.at[self.slot(key)],
            device_id=target,
            device_id_type=MESH_ID,
        ).wait_recv()

    def finish(self):
        for copy in self.sent:
            copy.wait_send()


AG_COPIES = 62


def gather_kernel(up_ref, dn_ref, gu_ref, gd_ref, own_sem, send_sem, recv_sem):
    spot = Spot()
    mine = (up_ref, dn_ref)
    full = (gu_ref, gd_ref)
    first_p, first_m = {"fsdp": spot.owner(1, 0)}, {"fsdp": spot.owner(3, 0)}
    second_p, second_m = {"fsdp": spot.owner(0, 1)}, {"fsdp": spot.owner(0, 3)}
    other = {"fsdp": spot.sibling()}
    greet([first_p, first_m, second_p, second_m, other])
    mail = Mail(send_sem, recv_sem)
    me = spot.owner(0, 0)

    def held(i, j, h):
        return mine[h] if (i, j) == (0, 0) else full[h].at[spot.owner(i, j)]

    def place(i, j, h):
        return full[h].at[spot.owner(i, j)]

    def arrive(i, j, h, key, source):
        mail.wait(place(i, j, h), key, source)

    def share(i, j, h):
        mail.send(held(i, j, h), place(i, j, h), other, ("sib", i, j, h))

    def second(i, h):
        mail.send(held(i, 0, h), place(i, 0, h), second_p, ("sec", i, 3, h))
        mail.send(held(i, 0, h), place(i, 0, h), second_m, ("sec", i, 1, h))

    keeps = [pltpu.make_async_copy(mine[h], full[h].at[me], own_sem.at[h]) for h in (0, 1)]
    for h in (0, 1):
        mail.send(mine[h], place(0, 0, h), first_p, ("fst", 3, h))
        mail.send(mine[1 - h], place(0, 0, 1 - h), first_m, ("fst", 1, 1 - h))
    for h in (0, 1):
        second(0, h)
    for h in (0, 1):
        share(0, 0, h)
        keeps[h].start()
    arrive(3, 0, 0, ("fst", 3, 0), first_m)
    mail.send(held(3, 0, 0), place(3, 0, 0), first_p, ("fst", 2, 0))
    arrive(1, 0, 1, ("fst", 1, 1), first_p)
    mail.send(held(1, 0, 1), place(1, 0, 1), first_m, ("fst", 2, 1))
    second(3, 0)
    second(1, 1)
    share(3, 0, 0)
    share(1, 0, 1)
    arrive(3, 0, 1, ("fst", 3, 1), first_m)
    second(3, 1)
    share(3, 0, 1)
    arrive(1, 0, 0, ("fst", 1, 0), first_p)
    second(1, 0)
    share(1, 0, 0)
    arrive(2, 0, 0, ("fst", 2, 0), first_m)
    second(2, 0)
    share(2, 0, 0)
    arrive(2, 0, 1, ("fst", 2, 1), first_p)
    second(2, 1)
    share(2, 0, 1)
    for i in (0, 3, 1, 2):
        arrive(i, 3, 0, ("sec", i, 3, 0), second_m)
        mail.send(held(i, 3, 0), place(i, 3, 0), second_p, ("sec", i, 2, 0))
        share(i, 3, 0)
        arrive(i, 1, 1, ("sec", i, 1, 1), second_p)
        mail.send(held(i, 1, 1), place(i, 1, 1), second_m, ("sec", i, 2, 1))
        share(i, 1, 1)
        arrive(i, 3, 1, ("sec", i, 3, 1), second_m)
        share(i, 3, 1)
        arrive(i, 1, 0, ("sec", i, 1, 0), second_p)
        share(i, 1, 0)
    for i in (0, 3, 1, 2):
        arrive(i, 2, 0, ("sec", i, 2, 0), second_m)
        share(i, 2, 0)
        arrive(i, 2, 1, ("sec", i, 2, 1), second_p)
        share(i, 2, 1)
    for i in range(RING):
        for j in range(RING):
            for h in (0, 1):
                mail.wait(full[h].at[spot.owner(i, j, 1 - spot.c)], ("sib", i, j, h), other)
    for keep in keeps:
        keep.wait()
    mail.finish()
    assert len(mail.sent) == len(mail.keys) == AG_COPIES


def gather_weights(up, dn):
    owners = 2 * RING * RING
    full = jax.ShapeDtypeStruct((owners,) + up.shape, up.dtype)
    return pl.pallas_call(
        gather_kernel,
        out_shape=(full, full),
        in_specs=[pl.BlockSpec(memory_space=pl.ANY)] * 2,
        out_specs=(pl.BlockSpec(memory_space=pl.ANY),) * 2,
        scratch_shapes=[
            pltpu.SemaphoreType.DMA((2,)),
            pltpu.SemaphoreType.DMA((AG_COPIES,)),
            pltpu.SemaphoreType.DMA((AG_COPIES,)),
        ],
        compiler_params=pltpu.CompilerParams(collective_id=0, has_side_effects=True),
        name="gather_weights",
    )(up, dn)


NT = (((1,), (1,)), ((), ()))
TN = (((0,), (0,)), ((), ()))
NN = (((1,), (0,)), ((), ()))


def mm(a, b, dims):
    return lax.dot_general(a, b, dims, preferred_element_type=F32)


UNROLL = 2


def layer_kernel(
    rows, cols, counts,
    x_hbm, dy_hbm, up_hbm, dn_hbm,
    out_hbm, in_hbm, pu_hbm, pd_hbm,
    x, dy, up, dn, out, inp, hid, pgr, pu, pd, acc,
    col_at, row_at, by_col, by_row, sem,
):
    total = rows.shape[0]
    tok, width = x_hbm.shape
    row_blocks = width // EDGE
    col_blocks = col_at.shape[0] - 2
    loads = [
        pltpu.make_async_copy(src, dst, sem.at[n])
        for n, (src, dst) in enumerate(((x_hbm, x), (dy_hbm, dy), (up_hbm, up), (dn_hbm, dn)))
    ]
    for load in loads:
        load.start()

    def clear(ref):
        def step(n, carry):
            ref[n] = 0
            return carry
        lax.fori_loop(0, ref.shape[0], step, 0)

    clear(col_at)
    clear(row_at)

    def live(k):
        return lax.rem(k, SLOTS) < counts[k // SLOTS]

    def count(k, carry):
        @pl.when(live(k))
        def _():
            col_at[cols[k] + 2] = col_at[cols[k] + 2] + 1
            row_at[rows[k] + 2] = row_at[rows[k] + 2] + 1
        return carry

    lax.fori_loop(0, total, count, 0)

    def prefix(ref):
        def step(n, carry):
            ref[n] = ref[n] + ref[n - 1]
            return carry
        lax.fori_loop(1, ref.shape[0], step, 0)

    prefix(col_at)
    prefix(row_at)
    n_live = col_at[col_blocks + 1]

    def order(k, carry):
        @pl.when(live(k))
        def _():
            c, r = cols[k] + 1, rows[k] + 1
            by_col[col_at[c]] = k
            col_at[c] = col_at[c] + 1
            by_row[row_at[r]] = k
            row_at[r] = row_at[r] + 1
        return carry

    lax.fori_loop(0, total, order, 0)
    for u in range(UNROLL):
        by_col[n_live + u] = by_col[n_live - 1]
        by_row[n_live + u] = by_row[n_live - 1]

    def zero_cols(b, carry):
        at = pl.ds(pl.multiple_of(b * EDGE, EDGE), EDGE)
        out[:, at] = jnp.zeros((tok, EDGE), BF16)
        inp[:, at] = jnp.zeros((tok, EDGE), BF16)
        return carry

    lax.fori_loop(0, row_blocks, zero_cols, 0)

    def zero_dead(k, carry):
        @pl.when(jnp.logical_not(live(k)))
        def _():
            pu[k] = jnp.zeros((EDGE, EDGE), BF16)
            pd[k] = jnp.zeros((EDGE, EDGE), BF16)
        return carry

    lax.fori_loop(0, total, zero_dead, 0)
    for load in loads:
        load.wait()

    def block(b):
        return pl.ds(pl.multiple_of(b * EDGE, EDGE), EDGE)

    steps = (n_live + UNROLL - 1) // UNROLL

    def forward(step, carry):
        pre, back = acc[0], acc[1]
        for u in range(UNROLL):
            s = step * UNROLL + u
            k = by_col[s]
            at = block(rows[k])
            first = jnp.logical_or(s == 0, cols[by_col[jnp.maximum(s - 1, 0)]] != cols[k])
            pre = jnp.where(first, 0.0, pre) + mm(x[:, at], up[k], NN)
            back = jnp.where(first, 0.0, back) + mm(dy[:, at], dn[k], NT)
            value, slope = gelu_parts(pre)
            hid[s] = value.astype(BF16)
            pgr[s] = (back * slope).astype(BF16)
        acc[0] = pre
        acc[1] = back
        return carry

    lax.fori_loop(0, steps, forward, 0)

    def backward(step, carry):
        o, g = acc[0], acc[1]
        for u in range(UNROLL):
            t = step * UNROLL + u
            k = by_row[t]
            r = rows[k]
            at = block(r)
            to = block(jnp.where(t < n_live, r, row_blocks))
            first = jnp.logical_or(t == 0, rows[by_row[jnp.maximum(t - 1, 0)]] != r)
            last = col_at[cols[k] + 1] - 1
            h, p = hid[last], pgr[last]
            o = jnp.where(first, 0.0, o) + mm(h, dn[k], NN)
            g = jnp.where(first, 0.0, g) + mm(p, up[k], NT)
            out[:, to] = o.astype(BF16)
            inp[:, to] = g.astype(BF16)
            pu[k] = mm(x[:, at], p, TN).astype(BF16)
            pd[k] = mm(h, dy[:, at], TN).astype(BF16)
        acc[0] = o
        acc[1] = g
        return carry

    lax.fori_loop(0, steps, backward, 0)
    stores = [
        pltpu.make_async_copy(src, dst, sem.at[n])
        for n, (src, dst) in enumerate((
            (out.at[:, pl.ds(0, width)], out_hbm), (inp.at[:, pl.ds(0, width)], in_hbm),
            (pu, pu_hbm), (pd, pd_hbm),
        ))
    ]
    for store in stores:
        store.start()
    for store in stores:
        store.wait()


def local_layer(rows, cols, counts, x, dy, up, dn, col_blocks):
    tok, width = x.shape
    total = rows.shape[0]
    any_spec = pl.BlockSpec(memory_space=pl.ANY)
    smem_spec = pl.BlockSpec(memory_space=pltpu.SMEM)
    part = jax.ShapeDtypeStruct((total, EDGE, EDGE), BF16)
    return pl.pallas_call(
        layer_kernel,
        out_shape=(
            jax.ShapeDtypeStruct((tok, width), BF16),
            jax.ShapeDtypeStruct((tok, width), BF16),
            part,
            part,
        ),
        in_specs=[smem_spec] * 3 + [any_spec] * 4,
        out_specs=(any_spec,) * 4,
        scratch_shapes=[
            pltpu.VMEM((tok, width), BF16),
            pltpu.VMEM((tok, width), BF16),
            pltpu.VMEM((total, EDGE, EDGE), BF16),
            pltpu.VMEM((total, EDGE, EDGE), BF16),
            pltpu.VMEM((tok, width + EDGE), BF16),
            pltpu.VMEM((tok, width + EDGE), BF16),
            pltpu.VMEM((total + UNROLL, tok, EDGE), BF16),
            pltpu.VMEM((total + UNROLL, tok, EDGE), BF16),
            pltpu.VMEM((total, EDGE, EDGE), BF16),
            pltpu.VMEM((total, EDGE, EDGE), BF16),
            pltpu.VMEM((2, tok, EDGE), F32),
            pltpu.SMEM((col_blocks + 2,), jnp.int32),
            pltpu.SMEM((width // EDGE + 2,), jnp.int32),
            pltpu.SMEM((total + UNROLL,), jnp.int32),
            pltpu.SMEM((total + UNROLL,), jnp.int32),
            pltpu.SemaphoreType.DMA((4,)),
        ],
        compiler_params=pltpu.CompilerParams(vmem_limit_bytes=56 << 20),
        name="local_layer",
    )(rows, cols, counts, x, dy, up.reshape(total, EDGE, EDGE), dn.reshape(total, EDGE, EDGE))


RS_COPIES = 66


def scatter_kernel(
    scale, pu_hbm, pd_hbm, ug_ref, dg_ref,
    own, sib, mid, got_m, got_p, r_bf, r_f32, mid2, fin_m, fin_p, zsend, zrecv,
    own_sem, send_sem, recv_sem,
):
    spot = Spot()
    part = (pu_hbm, pd_hbm)
    final = (ug_ref, dg_ref)
    first_p, first_m = {"fsdp": spot.owner(1, 0)}, {"fsdp": spot.owner(3, 0)}
    second_p, second_m = {"fsdp": spot.owner(0, 1)}, {"fsdp": spot.owner(0, 3)}
    other = {"fsdp": spot.sibling()}
    z_a = {"dp": spot.z + 1 - 2 * lax.rem(spot.z, 2)}
    z_b = {"dp": RING - 1 - spot.z}
    greet([first_p, first_m, second_p, second_m, other, z_a, z_b])
    mail = Mail(send_sem, recv_sem)
    order = [(i, j, h) for j in (2, 1, 3, 0) for i in (2, 1, 3, 0) for h in (0, 1)]
    loads = {}
    for n, (i, j, h) in enumerate(order):
        at = i * RING + j
        theirs = spot.owner(i, j, 1 - spot.c)
        mail.send(part[h].at[theirs], sib.at[h, at], other, ("sib", i, j, h))
        loads[i, j, h] = pltpu.make_async_copy(
            part[h].at[spot.owner(i, j)], own.at[h, at], own_sem.at[n]
        )
        loads[i, j, h].start()

    def pair(i, j, h):
        at = i * RING + j
        loads[i, j, h].wait()
        mail.wait(sib.at[h, at], ("sib", i, j, h), other)
        return own[h, at].astype(F32) + sib[h, at].astype(F32)

    def keep(i, j, h, value):
        at = i * RING + j
        own[h, at] = value.astype(BF16)
        return own.at[h, at]

    ring = (2, 1, 3, 0)
    for i in ring:
        mail.send(keep(i, 2, 0, pair(i, 2, 0)), mid.at[i, 0], second_p, ("mid", i, 0))
        mail.send(keep(i, 2, 1, pair(i, 2, 1)), mid.at[i, 1], second_m, ("mid", i, 1))
    for i in ring:
        mail.send(keep(i, 1, 1, pair(i, 1, 1)), got_m.at[i, 1], second_p, ("m", i, 1))
        mail.send(keep(i, 3, 0, pair(i, 3, 0)), got_p.at[i, 0], second_m, ("p", i, 0))
        near = pair(i, 1, 0)
        mail.wait(mid.at[i, 0], ("mid", i, 0), second_m)
        near = near + mid[i, 0].astype(F32)
        mail.send(keep(i, 1, 0, near), got_m.at[i, 0], second_p, ("m", i, 0))
        near = pair(i, 3, 1)
        mail.wait(mid.at[i, 1], ("mid", i, 1), second_p)
        near = near + mid[i, 1].astype(F32)
        mail.send(keep(i, 3, 1, near), got_p.at[i, 1], second_m, ("p", i, 1))

    def ring_sum(i, h):
        value = pair(i, 0, h)
        mail.wait(got_m.at[i, h], ("m", i, h), second_m)
        mail.wait(got_p.at[i, h], ("p", i, h), second_p)
        return value + got_m[i, h].astype(F32) + got_p[i, h].astype(F32)

    for n, (i, h, dst, target, key) in enumerate((
        (2, 0, mid2.at[0], first_p, ("mid2", 0)),
        (2, 1, mid2.at[1], first_m, ("mid2", 1)),
        (1, 1, fin_m.at[1], first_p, ("fm", 1)),
        (3, 0, fin_p.at[0], first_m, ("fp", 0)),
    )):
        r_bf[n] = ring_sum(i, h).astype(BF16)
        mail.send(r_bf.at[n], dst, target, key)
    for n, (i, h, dst, target, key, source) in enumerate((
        (1, 0, fin_m.at[0], first_p, ("fm", 0), first_m),
        (3, 1, fin_p.at[1], first_m, ("fp", 1), first_p),
    )):
        r_f32[n] = ring_sum(i, h)
        mail.wait(mid2.at[h], ("mid2", h), source)
        r_bf[4 + n] = (r_f32[n] + mid2[h].astype(F32)).astype(BF16)
        mail.send(r_bf.at[4 + n], dst, target, key)
    for h in (0, 1):
        r_f32[h] = ring_sum(0, h)
    for h in (0, 1):
        mail.wait(fin_m.at[h], ("fm", h), first_m)
        mail.wait(fin_p.at[h], ("fp", h), first_p)
        value = r_f32[h] + fin_m[h].astype(F32) + fin_p[h].astype(F32)
        zsend[0, h] = value.astype(BF16)
        mail.send(zsend.at[0, h], zrecv.at[0, h], (z_a, z_b)[h], ("z", 0, h))
    for h in (0, 1):
        mail.wait(zrecv.at[0, h], ("z", 0, h), (z_a, z_b)[h])
        value = zsend[0, h].astype(F32) + zrecv[0, h].astype(F32)
        zsend[1, h] = value.astype(BF16)
        mail.send(zsend.at[1, h], zrecv.at[1, h], (z_b, z_a)[h], ("z", 1, h))
    for h in (0, 1):
        mail.wait(zrecv.at[1, h], ("z", 1, h), (z_b, z_a)[h])
        value = zsend[1, h].astype(F32) + zrecv[1, h].astype(F32)
        final[h][...] = value * scale
    mail.finish()
    assert len(mail.sent) == len(mail.keys) == RS_COPIES


def scatter_grads(pu, pd, scale):
    owners = 2 * RING * RING
    piece = (SLOTS, EDGE, EDGE)
    grad = jax.ShapeDtypeStruct(piece, F32)
    vmem = pl.BlockSpec(memory_space=pltpu.VMEM)
    return pl.pallas_call(
        functools.partial(scatter_kernel, scale),
        out_shape=(grad, grad),
        in_specs=[pl.BlockSpec(memory_space=pl.ANY)] * 2,
        out_specs=(vmem, vmem),
        scratch_shapes=[
            pltpu.VMEM((2, RING * RING) + piece, BF16),
            pltpu.VMEM((2, RING * RING) + piece, BF16),
            pltpu.VMEM((RING, 2) + piece, BF16),
            pltpu.VMEM((RING, 2) + piece, BF16),
            pltpu.VMEM((RING, 2) + piece, BF16),
            pltpu.VMEM((6,) + piece, BF16),
            pltpu.VMEM((2,) + piece, F32),
            pltpu.VMEM((2,) + piece, BF16),
            pltpu.VMEM((2,) + piece, BF16),
            pltpu.VMEM((2,) + piece, BF16),
            pltpu.VMEM((2, 2) + piece, BF16),
            pltpu.VMEM((2, 2) + piece, BF16),
            pltpu.SemaphoreType.DMA((2 * RING * RING,)),
            pltpu.SemaphoreType.DMA((RS_COPIES,)),
            pltpu.SemaphoreType.DMA((RS_COPIES,)),
        ],
        compiler_params=pltpu.CompilerParams(
            collective_id=1, has_side_effects=True, vmem_limit_bytes=48 << 20
        ),
        name="scatter_grads",
    )(pu.reshape((owners,) + piece), pd.reshape((owners,) + piece))


COL_BLOCKS = 192


def on_device(tokens, cotangent, up_w, dn_w, block_rows, block_cols, owner_counts):
    devices = lax.axis_size("dp") * lax.axis_size("fsdp")
    scale = 1.0 / math.sqrt(tokens.shape[0] * devices)
    up_full, dn_full = gather_weights(up_w, dn_w)
    output, input_grad, up_part, dn_part = local_layer(
        block_rows, block_cols, owner_counts, tokens, cotangent, up_full, dn_full, COL_BLOCKS
    )
    up_grad, down_grad = scatter_grads(up_part, dn_part, scale)
    return output, input_grad, up_grad, down_grad


def solution(mesh):
    in_specs = (
        P(("dp", "fsdp"), None),
        P(("dp", "fsdp"), None),
        P("fsdp", None, None),
        P("fsdp", None, None),
        P(),
        P(),
        P(),
    )
    out_specs = (
        P(("dp", "fsdp"), None),
        P(("dp", "fsdp"), None),
        P("fsdp", None, None),
        P("fsdp", None, None),
    )
    return jax.shard_map(
        on_device, mesh=mesh, in_specs=in_specs, out_specs=out_specs, check_vma=False
    )
```

time: 449 us -> 116 us (0.26)
  matrix products: 316 us -> 0 us
  Pallas kernels: 0 us -> 110 us
  waiting for transfers between devices: 91.2 us -> 0 us
  local copies, waits for them, and re-layouts: 21 us -> 3.59 us
  between operations: 14.2 us -> 0.66 us
    dot_general x18 -> x0, matrix products: 316 us -> none  [the longest x4 119 us: spread_blocks(): jnp.einsum('sc,snj->cnj', table, contrib, preferred_element_type=jnp.floa...]
    pallas_call x0 -> x3, Pallas kernels: none -> 110 us  [the longest x1 39.3 us: scatter_grads(): pl.pallas_call(functools.partial(scatter_kernel, scale), out_shape=(grad,...]
    psum x1 -> x0, waiting for transfers between devices: 38.6 us -> none  [on_device(): up_grad, down_grad = lax.psum((up_local, down_local), 'dp')]
    reduce_scatter x2 -> x0, waiting for transfers between devices: 29.1 us -> none  [the longest x1 29.1 us: on_device(): lax.psum_scatter(jnp.einsum('snk,snj->skj', h_pick, dy_pick, preferred_el...]
    all_gather x2 -> x0, waiting for transfers between devices: 22.1 us -> none  [the longest x1 22.1 us: on_device(): up_whole = lax.all_gather(up_weight_blocks, 'fsdp', axis=0, tiled=True)]
    unnamed x18 -> x4, local copies, waits for them, and re-layouts: 9.8 us -> 3.59 us
    reshape x1 -> x0, local copies, waits for them, and re-layouts: 6.09 us -> none  [from_blocks(): blocks.transpose(1, 0, 2)]
    gather x4 -> x0, local copies, waits for them, and re-layouts: 5.08 us -> none  [the longest x1 1.4 us: on_device(): keep_mask = live_mask[slot_list].astype(jnp.float32)[:, None, None]]
  transfers between devices with their start and end apart: 5 -> 0, of which waited for: 3 -> 0; matrix products, arithmetic and copies ran while one was open for 54% -> 0% of each run, Pallas kernels for 0% -> 0%
where the time goes in v1:
time: 116 us; the launch traced here: 114 us
  Pallas kernels  110 us (95%)
  local copies, waits for them, and re-layouts  3.59 us (3%)
    pallas_call x1, Pallas kernels, scatter_grads(): pl.pallas_call(functools.partial(scatter_kernel, scale), out_shape=(grad,...  39.3 us
    pallas_call x1, Pallas kernels, local_layer(): pl.pallas_call(layer_kernel, out_shape=(jax.ShapeDtypeStruct((tok, width)...  38.8 us
    pallas_call x1, Pallas kernels, gather_weights(): pl.pallas_call(gather_kernel, out_shape=(full, full), in_specs=[pl.BlockS...  31.8 us
    unnamed x4, local copies, waits for them, and re-layouts  3.59 us

profile of v1, /device:TPU:1, one launch (start us, length us, event | category | flops | bytes accessed | tf_op | source)
XLA Modules:
  0.0 114.2 jit_solution(15397061520583551014)
XLA Ops:
  0.6 31.8 %gather_weights.1 = (bf16[32,4,128,128]{3,2,1,0:T(8,128)(2,1)}, bf16[32,4,128,128]{3,2,1,0:T(8,128)(2,1)}) custom-call(bf16[4,128,128]{2,1,0:T(8,128)(2,1)} %up_ref.1, bf16[4,128,128]{2,1,0:T(8,128)(2,1)} %dn_ref.1), custom_call_target="tpu_custom_call" | custom-call | tf_op jit(solution)/shard_map/gather_weights/pallas_call | solution.py:180
  32.4 38.8 %local_layer.1 = (bf16[256,6144]{1,0:T(8,128)(2,1)}, bf16[256,6144]{1,0:T(8,128)(2,1)}, bf16[128,128,128]{2,1,0:T(8,128)(2,1)}, bf16[128,128,128]{2,1,0:T(8,128)(2,1)}) custom-call(s32[128]{0:T(128)} %rows.1, s32[128]{0:T(128)} %cols.1, s32[32]{0:T(128)} %counts.1, bf16[256,6144]{1,0:T(8,128)(2,1)} %x_hbm.1, bf16[256,6144]{1,0:T(8,128)(2,1)} %dy_hbm.1, ...), custom_call_target="tpu_custom_call" | custom-call | tf_op jit(solution)/shard_map/local_layer/pallas_call | solution.py:354
  71.3 0.0 copy-start
  71.3 2.2 %copy-done = bf16[128,128,128]{2,1,0:T(8,128)(2,1)S(1)} copy-done((bf16[128,128,128]{2,1,0:T(8,128)(2,1)S(1)}, bf16[128,128,128]{2,1,0:T(8,128)(2,1)}, u32[]{:S(2)}) %copy-start) | copy-done | bytes 4194328
  73.5 39.3 %scatter_grads.1 = (f32[4,128,128]{2,1,0:T(8,128)S(1)}, f32[4,128,128]{2,1,0:T(8,128)S(1)}) custom-call(bf16[32,4,128,128]{3,2,1,0:T(8,128)(2,1)S(1)} %bitcast.4, bf16[32,4,128,128]{3,2,1,0:T(8,128)(2,1)} %bitcast.7), custom_call_target="tpu_custom_call" | custom-call | tf_op jit(solution)/shard_map/scatter_grads/pallas_call | solution.py:491
  112.8 0.7 copy.13
  113.5 0.7 copy.14
Async XLA Ops:
  71.3 2.2 %copy-start = (bf16[128,128,128]{2,1,0:T(8,128)(2,1)S(1)}, bf16[128,128,128]{2,1,0:T(8,128)(2,1)}, u32[]{:S(2)}) copy-start(bf16[128,128,128]{2,1,0:T(8,128)(2,1)} %get-tuple-element.16) | copy-start | bytes 12582916

commit v2 on v1

v2 whole, which is shorter than its diff:
```python
import functools
import math

import jax
import jax.numpy as jnp
from jax import lax
from jax.experimental import pallas as pl
from jax.experimental.pallas import tpu as pltpu
from jax.sharding import PartitionSpec as P

EDGE = 128
SLOTS = 4
RING = 4
MESH_ID = pl.DeviceIdType.MESH
BF16 = jnp.bfloat16
F32 = jnp.float32

gelu_scale = 0.7978845608028654
cubic_coef = 0.044715


def gelu_parts(values):
    inner_arg = gelu_scale * (values + cubic_coef * values * values * values)
    tanh_val = jnp.tanh(inner_arg)
    gelu_value = 0.5 * values * (1.0 + tanh_val)
    gelu_slope = 0.5 * (1.0 + tanh_val) + 0.5 * values * (
        1.0 - tanh_val * tanh_val
    ) * gelu_scale * (1.0 + 3.0 * cubic_coef * values * values)
    return gelu_value, gelu_slope


class Spot:
    def __init__(self):
        me = lax.axis_index("fsdp")
        self.z = lax.axis_index("dp")
        self.c = lax.rem(me, 2)
        self.y = lax.rem(me // 2, RING)
        self.x = me // (2 * RING)

    def owner(self, i, j, c=None):
        c = self.c if c is None else c
        x = lax.rem(self.x + i * (1 - c) + j * c, RING)
        y = lax.rem(self.y + i * c + j * (1 - c), RING)
        return (x * RING + y) * 2 + c

    def sibling(self):
        return (self.x * RING + self.y) * 2 + (1 - self.c)


def greet(targets):
    barrier = pltpu.get_barrier_semaphore()
    for target in targets:
        pl.semaphore_signal(barrier, inc=1, device_id=target, device_id_type=MESH_ID)
    pl.semaphore_wait(barrier, len(targets))


class Mail:
    def __init__(self, send_sem, recv_sem):
        self.send_sem, self.recv_sem = send_sem, recv_sem
        self.keys, self.sent = {}, []

    def slot(self, key):
        return self.keys.setdefault(key, len(self.keys))

    def send(self, src, dst, target, key):
        copy = pltpu.make_async_remote_copy(
            src_ref=src,
            dst_ref=dst,
            send_sem=self.send_sem.at[len(self.sent)],
            recv_sem=self.recv_sem.at[self.slot(key)],
            device_id=target,
            device_id_type=MESH_ID,
        )
        copy.start()
        self.sent.append(copy)

    def wait(self, dst, key, target):
        pltpu.make_async_remote_copy(
            src_ref=dst,
            dst_ref=dst,
            send_sem=self.send_sem.at[0],
            recv_sem=self.recv_sem.at[self.slot(key)],
            device_id=target,
            device_id_type=MESH_ID,
        ).wait_recv()

    def finish(self):
        for copy in self.sent:
            copy.wait_send()

    def copy_at(self, src, dst, target, n):
        return pltpu.make_async_remote_copy(
            src_ref=src,
            dst_ref=dst,
            send_sem=self.send_sem.at[n],
            recv_sem=self.recv_sem.at[n],
            device_id=target,
            device_id_type=MESH_ID,
        )

    def send_at(self, src, dst, target, n):
        self.copy_at(src, dst, target, n).start()

    def wait_at(self, dst, target, n):
        self.copy_at(dst, dst, target, n).wait_recv()

    def sent_at(self, src, target, n):
        self.copy_at(src, src, target, n).wait_send()


VM_K1 = 8 << 20
AG_COPIES = 62
SLOT_TOTAL = 128
DEAD = SLOT_TOTAL
BY_COL, BY_ROW, LAST, LIVE = 0, 1, 2, 3


def slot_tables(rows_ref, cols_ref, counts, tab_ref):
    n = SLOT_TOTAL
    lane = lax.broadcasted_iota(jnp.int32, (n, n), 1)
    sub = lax.broadcasted_iota(jnp.int32, (n, n), 0)
    lane_owner = lax.broadcasted_iota(jnp.int32, (8, n), 1) // SLOTS
    held = jnp.zeros((8, n), jnp.int32)
    for o in range(n // SLOTS):
        held = jnp.where(lane_owner == o, counts[o], held)
    lane_f, sub_f = lane.astype(F32), sub.astype(F32)

    def spread(row):
        across = jnp.broadcast_to(row.astype(F32), (n, n))
        return across, across.T

    held_l, held_s = spread(held[0:1])
    slot_l = lax.rem(lane, SLOTS).astype(F32)
    slot_s = lax.rem(sub, SLOTS).astype(F32)
    live_l = jnp.where(slot_l < held_l, 1.0, 0.0)
    live_s = jnp.where(slot_s < held_s, 1.0, 0.0)

    def order(key_l, key_s):
        tie = jnp.where(key_l == key_s, jnp.where(lane < sub, live_l, 0.0), 0.0)
        rank = jnp.sum(jnp.where(key_l < key_s, live_l, tie), axis=1, keepdims=True)
        hit = jnp.where(rank == lane_f, live_s, 0.0)
        return jnp.sum(hit * sub_f, axis=0, keepdims=True)

    col_l, col_s = spread(cols_ref[...])
    row_l, row_s = spread(rows_ref[...])
    upto = jnp.sum(jnp.where(col_s <= col_l, live_s, 0.0), axis=0, keepdims=True)
    last = jnp.where(live_l[0:1] > 0.5, upto - 1.0, float(DEAD))
    number = jnp.sum(live_s, axis=0, keepdims=True)
    for at, row in (
        (BY_COL, order(col_l, col_s)), (BY_ROW, order(row_l, row_s)), (LAST, last), (LIVE, number)
    ):
        tab_ref[at:at + 1, :] = row.astype(jnp.int32)


def gather_kernel(
    rows_ref, cols_ref, counts, up_ref, dn_ref, x_hbm, dy_hbm,
    gu_ref, gd_ref, x_ref, dy_ref, tab_ref, own_sem, send_sem, recv_sem,
):
    spot = Spot()
    mine = (up_ref, dn_ref)
    full = (gu_ref, gd_ref)
    first_p, first_m = {"fsdp": spot.owner(1, 0)}, {"fsdp": spot.owner(3, 0)}
    second_p, second_m = {"fsdp": spot.owner(0, 1)}, {"fsdp": spot.owner(0, 3)}
    other = {"fsdp": spot.sibling()}
    greet([first_p, first_m, second_p, second_m, other])
    mail = Mail(send_sem, recv_sem)
    me = spot.owner(0, 0)

    def held(i, j, h):
        return mine[h] if (i, j) == (0, 0) else full[h].at[spot.owner(i, j)]

    def place(i, j, h):
        return full[h].at[spot.owner(i, j)]

    def arrive(i, j, h, key, source):
        mail.wait(place(i, j, h), key, source)

    def share(i, j, h):
        mail.send(held(i, j, h), place(i, j, h), other, ("sib", i, j, h))

    def second(i, h):
        mail.send(held(i, 0, h), place(i, 0, h), second_p, ("sec", i, 3, h))
        mail.send(held(i, 0, h), place(i, 0, h), second_m, ("sec", i, 1, h))

    keeps = [
        pltpu.make_async_copy(src, dst, own_sem.at[n])
        for n, (src, dst) in enumerate((
            (up_ref, gu_ref.at[me]), (dn_ref, gd_ref.at[me])
        ))
    ]
    blocks = x_ref.shape[0]

    def cut(b, carry):
        at = pl.ds(pl.multiple_of(b * EDGE, EDGE), EDGE)
        pltpu.make_async_copy(x_hbm.at[:, at], x_ref.at[b], own_sem.at[2]).start()
        pltpu.make_async_copy(dy_hbm.at[:, at], dy_ref.at[b], own_sem.at[3]).start()
        return carry

    for h in (0, 1):
        mail.send(mine[h], place(0, 0, h), first_p, ("fst", 3, h))
        mail.send(mine[1 - h], place(0, 0, 1 - h), first_m, ("fst", 1, 1 - h))
    for h in (0, 1):
        second(0, h)
    for h in (0, 1):
        share(0, 0, h)
    for keep in keeps:
        keep.start()
    lax.fori_loop(0, blocks, cut, 0)
    slot_tables(rows_ref, cols_ref, counts, tab_ref)
    arrive(3, 0, 0, ("fst", 3, 0), first_m)
    mail.send(held(3, 0, 0), place(3, 0, 0), first_p, ("fst", 2, 0))
    arrive(1, 0, 1, ("fst", 1, 1), first_p)
    mail.send(held(1, 0, 1), place(1, 0, 1), first_m, ("fst", 2, 1))
    second(3, 0)
    second(1, 1)
    share(3, 0, 0)
    share(1, 0, 1)
    arrive(3, 0, 1, ("fst", 3, 1), first_m)
    second(3, 1)
    share(3, 0, 1)
    arrive(1, 0, 0, ("fst", 1, 0), first_p)
    second(1, 0)
    share(1, 0, 0)
    arrive(2, 0, 0, ("fst", 2, 0), first_m)
    second(2, 0)
    share(2, 0, 0)
    arrive(2, 0, 1, ("fst", 2, 1), first_p)
    second(2, 1)
    share(2, 0, 1)
    for i in (0, 3, 1, 2):
        arrive(i, 3, 0, ("sec", i, 3, 0), second_m)
        mail.send(held(i, 3, 0), place(i, 3, 0), second_p, ("sec", i, 2, 0))
        share(i, 3, 0)
        arrive(i, 1, 1, ("sec", i, 1, 1), second_p)
        mail.send(held(i, 1, 1), place(i, 1, 1), second_m, ("sec", i, 2, 1))
        share(i, 1, 1)
        arrive(i, 3, 1, ("sec", i, 3, 1), second_m)
        share(i, 3, 1)
        arrive(i, 1, 0, ("sec", i, 1, 0), second_p)
        share(i, 1, 0)
    for i in (0, 3, 1, 2):
        arrive(i, 2, 0, ("sec", i, 2, 0), second_m)
        share(i, 2, 0)
        arrive(i, 2, 1, ("sec", i, 2, 1), second_p)
        share(i, 2, 1)
    for i in range(RING):
        for j in range(RING):
            for h in (0, 1):
                mail.wait(full[h].at[spot.owner(i, j, 1 - spot.c)], ("sib", i, j, h), other)
    for keep in keeps:
        keep.wait()
    pltpu.make_async_copy(x_ref, x_ref, own_sem.at[2]).wait()
    pltpu.make_async_copy(dy_ref, dy_ref, own_sem.at[3]).wait()
    mail.finish()
    assert len(mail.sent) == len(mail.keys) == AG_COPIES


def gather_weights(rows, cols, counts, up, dn, x, dy):
    owners = 2 * RING * RING
    any_spec = pl.BlockSpec(memory_space=pltpu.HBM)
    vmem_spec = pl.BlockSpec(memory_space=pltpu.VMEM)
    full = pltpu.VMEM((owners,) + up.shape, up.dtype)
    cut = pltpu.VMEM((x.shape[1] // EDGE, x.shape[0], EDGE), x.dtype)
    return pl.pallas_call(
        gather_kernel,
        out_shape=(
            full, full, cut, cut,
            jax.ShapeDtypeStruct((8, SLOT_TOTAL), jnp.int32),
        ),
        in_specs=[vmem_spec] * 2 + [pl.BlockSpec(memory_space=pltpu.SMEM)] + [any_spec] * 4,
        out_specs=(vmem_spec,) * 5,
        scratch_shapes=[
            pltpu.SemaphoreType.DMA((4,)),
            pltpu.SemaphoreType.DMA((AG_COPIES,)),
            pltpu.SemaphoreType.DMA((AG_COPIES,)),
        ],
        compiler_params=pltpu.CompilerParams(
            collective_id=0, has_side_effects=True, vmem_limit_bytes=VM_K1
        ),
        name="gather_weights",
    )(rows.reshape(1, SLOT_TOTAL), cols.reshape(1, SLOT_TOTAL), counts,
      in_hbm(up), in_hbm(dn), in_hbm(x), in_hbm(dy))


NT = (((1,), (1,)), ((), ()))
TN = (((0,), (0,)), ((), ()))
NN = (((1,), (0,)), ((), ()))


def mm(a, b, dims):
    return lax.dot_general(a, b, dims, preferred_element_type=F32)


UNROLL = 4


def layer_kernel(
    rows, cols, tab, x, dy, up, dn, out_hbm, in_hbm, hid, pgr, out, inp, acc, sem
):
    row_blocks, tok = x.shape[:2]
    width = row_blocks * EDGE
    n_live = tab[LIVE, 0]
    steps = (n_live + UNROLL - 1) // UNROLL

    def block(b):
        return pl.ds(pl.multiple_of(b * EDGE, EDGE), EDGE)

    hid[DEAD] = jnp.zeros((tok, EDGE), BF16)
    pgr[DEAD] = jnp.zeros((tok, EDGE), BF16)

    def forward(step, carry):
        pre, back = acc[0], acc[1]
        for u in range(UNROLL):
            s = step * UNROLL + u
            k = tab[BY_COL, jnp.minimum(s, n_live - 1)]
            before = tab[BY_COL, jnp.clip(s - 1, 0, n_live - 1)]
            r = rows[k]
            first = jnp.logical_or(s == 0, cols[before] != cols[k])
            pre = jnp.where(first, 0.0, pre) + mm(x[r], up[k], NN)
            back = jnp.where(first, 0.0, back) + mm(dy[r], dn[k], NT)
            value, slope = gelu_parts(pre)
            to = jnp.where(s < n_live, s, DEAD + 1)
            hid[to] = value.astype(BF16)
            pgr[to] = (back * slope).astype(BF16)
        acc[0] = pre
        acc[1] = back
        return carry

    lax.fori_loop(0, steps, forward, 0)

    def clear(b, carry):
        out[:, block(b)] = jnp.zeros((tok, EDGE), BF16)
        inp[:, block(b)] = jnp.zeros((tok, EDGE), BF16)
        return carry

    lax.fori_loop(0, row_blocks, clear, 0)

    def put(b, carry):
        pltpu.make_async_copy(out.at[:, block(b)], out_hbm.at[:, block(b)], sem.at[0]).start()
        pltpu.make_async_copy(inp.at[:, block(b)], in_hbm.at[:, block(b)], sem.at[1]).start()
        return carry

    def backward(step, done):
        o, g = acc[0], acc[1]
        for u in range(UNROLL):
            t = step * UNROLL + u
            k = tab[BY_ROW, jnp.minimum(t, n_live - 1)]
            r = rows[k]
            before = tab[BY_ROW, jnp.clip(t - 1, 0, n_live - 1)]
            to = block(jnp.where(t < n_live, r, row_blocks))
            first = jnp.logical_or(t == 0, rows[before] != r)
            last = tab[LAST, k]
            o = jnp.where(first, 0.0, o) + mm(hid[last], dn[k], NN)
            g = jnp.where(first, 0.0, g) + mm(pgr[last], up[k], NT)
            out[:, to] = o.astype(BF16)
            inp[:, to] = g.astype(BF16)
        acc[0] = o
        acc[1] = g
        upto = rows[tab[BY_ROW, jnp.minimum((step + 1) * UNROLL - 1, n_live - 1)]]
        lax.fori_loop(done, upto, put, 0)
        return upto

    done = lax.fori_loop(0, steps, backward, 0)
    lax.fori_loop(done, row_blocks, put, 0)
    whole = pl.ds(0, width)
    pltpu.make_async_copy(out.at[:, whole], out_hbm, sem.at[0]).wait()
    pltpu.make_async_copy(inp.at[:, whole], in_hbm, sem.at[1]).wait()


def local_layer(rows, cols, tab, x, dy, up, dn):
    row_blocks, tok = x.shape[:2]
    width = row_blocks * EDGE
    any_spec = pl.BlockSpec(memory_space=pl.ANY)
    smem_spec = pl.BlockSpec(memory_space=pltpu.SMEM)
    vmem_spec = pl.BlockSpec(memory_space=pltpu.VMEM)
    kept = pltpu.VMEM((SLOT_TOTAL + 2, tok, EDGE), BF16)
    result = jax.ShapeDtypeStruct((tok, width), BF16)
    return pl.pallas_call(
        layer_kernel,
        out_shape=(result, result, kept, kept),
        in_specs=[smem_spec] * 3 + [vmem_spec] * 4,
        out_specs=(any_spec,) * 2 + (vmem_spec,) * 2,
        scratch_shapes=[
            pltpu.VMEM((tok, width + EDGE), BF16),
            pltpu.VMEM((tok, width + EDGE), BF16),
            pltpu.VMEM((2, tok, EDGE), F32),
            pltpu.SemaphoreType.DMA((2,)),
        ],
        compiler_params=pltpu.CompilerParams(vmem_limit_bytes=VM_K2),
        name="local_layer",
    )(
        rows, cols, tab, in_vmem(x), in_vmem(dy),
        in_vmem(up.reshape(SLOT_TOTAL, EDGE, EDGE)), in_vmem(dn.reshape(SLOT_TOTAL, EDGE, EDGE)),
    )


VM_K2 = 16 << 20


def in_hbm(array):
    return pltpu.with_memory_space_constraint(array, pltpu.HBM)


def in_vmem(array):
    return pltpu.with_memory_space_constraint(array, pltpu.VMEM)


RS_COPIES = 66
VM_K3 = 26 << 20


def scatter_kernel(
    scale, rows, tab, x, dy, hid, pgr, ug_ref, dg_ref,
    stage, own, sib, mid, got_m, got_p, r_bf, r_f32, mid2, fin_m, fin_p, zsend, zrecv,
    send_sem, recv_sem,
):
    spot = Spot()
    final = (ug_ref, dg_ref)
    first_p, first_m = {"fsdp": spot.owner(1, 0)}, {"fsdp": spot.owner(3, 0)}
    second_p, second_m = {"fsdp": spot.owner(0, 1)}, {"fsdp": spot.owner(0, 3)}
    other = {"fsdp": spot.sibling()}
    z_a = {"dp": spot.z + 1 - 2 * lax.rem(spot.z, 2)}
    z_b = {"dp": RING - 1 - spot.z}
    greet([first_p, first_m, second_p, second_m, other, z_a, z_b])
    mail = Mail(send_sem, recv_sem)

    def partial(owner, h, q):
        k = owner * SLOTS + q
        if h == 0:
            return mm(x[rows[k]], pgr[tab[LAST, k]], TN)
        return mm(hid[tab[LAST, k]], dy[rows[k]], TN)

    def give(j):
        def step(n, carry):
            i = turn(n)
            at = i * RING + j
            for h in (0, 1):
                for q in range(SLOTS):
                    stage[h, at, q] = partial(spot.owner(i, j, 1 - spot.c), h, q).astype(BF16)
                mail.send_at(stage.at[h, at], sib.at[h, at], other, 2 * at + h)
            return carry
        lax.fori_loop(0, RING, step, 0)

    def pair(i, j, h, then, *more):
        at = i * RING + j
        mail.wait_at(sib.at[h, at], other, 2 * at + h)
        for q in range(SLOTS):
            value = partial(spot.owner(i, j), h, q) + sib[h, at, q].astype(F32)
            for ref in more:
                value = value + ref[q].astype(F32)
            then(q, value)

    def keep(i, j, h, *more):
        at = i * RING + j

        def then(q, value):
            own[h, at, q] = value.astype(BF16)

        pair(i, j, h, then, *more)
        return own.at[h, at]

    base = 2 * RING * RING
    give(2)
    give(3)

    def far(n, carry):
        i = turn(n)
        mail.send_at(keep(i, 2, 0), mid.at[i, 0], second_p, base + i)
        mail.send_at(keep(i, 2, 1), mid.at[i, 1], second_m, base + RING + i)
        return carry

    lax.fori_loop(0, RING, far, 0)
    give(1)
    base += 2 * RING

    def near(n, carry):
        i = turn(n)
        mail.send_at(keep(i, 1, 1), got_m.at[i, 1], second_p, base + i)
        mail.send_at(keep(i, 3, 0), got_p.at[i, 0], second_m, base + RING + i)
        mail.wait_at(mid.at[i, 0], second_m, base - 2 * RING + i)
        mail.send_at(keep(i, 1, 0, mid.at[i, 0]), got_m.at[i, 0], second_p, base + 2 * RING + i)
        mail.wait_at(mid.at[i, 1], second_p, base - RING + i)
        mail.send_at(keep(i, 3, 1, mid.at[i, 1]), got_p.at[i, 1], second_m, base + 3 * RING + i)
        return carry

    lax.fori_loop(0, RING, near, 0)
    give(0)

    def ring_sum(i, h, then):
        mail.wait_at(got_m.at[i, h], second_m, base + (2 * RING, 0)[h] + i)
        mail.wait_at(got_p.at[i, h], second_p, base + (RING, 3 * RING)[h] + i)
        pair(i, 0, h, then, got_m.at[i, h], got_p.at[i, h])

    one = base + 4 * RING
    for n, (i, h, dst, target) in enumerate((
        (2, 0, mid2.at[0], first_p),
        (2, 1, mid2.at[1], first_m),
        (1, 1, fin_m.at[1], first_p),
        (3, 0, fin_p.at[0], first_m),
    )):
        def store(q, value):
            r_bf[n, q] = value.astype(BF16)

        ring_sum(i, h, store)
        mail.send_at(r_bf.at[n], dst, target, one + n)
    for n, (i, h, dst, target, source) in enumerate((
        (1, 0, fin_m.at[0], first_p, first_m),
        (3, 1, fin_p.at[1], first_m, first_p),
    )):
        def store(q, value):
            r_f32[n, q] = value

        ring_sum(i, h, store)
        mail.wait_at(mid2.at[h], source, one + h)
        r_bf[4 + n] = (r_f32[n] + mid2[h].astype(F32)).astype(BF16)
        mail.send_at(r_bf.at[4 + n], dst, target, one + 4 + n)
    for h in (0, 1):
        def store(q, value):
            r_f32[h, q] = value

        ring_sum(0, h, store)
    plane = one + 6
    for h in (0, 1):
        mail.wait_at(fin_m.at[h], first_m, one + (4, 2)[h])
        mail.wait_at(fin_p.at[h], first_p, one + (3, 5)[h])
        value = r_f32[h] + fin_m[h].astype(F32) + fin_p[h].astype(F32)
        zsend[0, h] = value.astype(BF16)
        mail.send_at(zsend.at[0, h], zrecv.at[0, h], (z_a, z_b)[h], plane + h)
    for h in (0, 1):
        mail.wait_at(zrecv.at[0, h], (z_a, z_b)[h], plane + h)
        value = zsend[0, h].astype(F32) + zrecv[0, h].astype(F32)
        zsend[1, h] = value.astype(BF16)
        mail.send_at(zsend.at[1, h], zrecv.at[1, h], (z_b, z_a)[h], plane + 2 + h)
    for h in (0, 1):
        mail.wait_at(zrecv.at[1, h], (z_b, z_a)[h], plane + 2 + h)
        value = zsend[1, h].astype(F32) + zrecv[1, h].astype(F32)
        final[h][...] = value * scale

    def sent(n, carry):
        mail.sent_at(stage.at[0, 0], other, n)
        return carry

    lax.fori_loop(0, RS_COPIES, sent, 0)


def turn(n):
    return lax.rem(2 + n * (n + 1) // 2, RING)


def scatter_grads(rows, tab, x, dy, hid, pgr, scale):
    piece = (SLOTS, EDGE, EDGE)
    grad = jax.ShapeDtypeStruct(piece, F32)
    vmem = pl.BlockSpec(memory_space=pltpu.VMEM)
    smem = pl.BlockSpec(memory_space=pltpu.SMEM)
    return pl.pallas_call(
        functools.partial(scatter_kernel, scale),
        out_shape=(grad, grad),
        in_specs=[smem] * 2 + [vmem] * 4,
        out_specs=(vmem, vmem),
        scratch_shapes=[
            pltpu.VMEM((2, RING * RING) + piece, BF16),
            pltpu.VMEM((2, RING * RING) + piece, BF16),
            pltpu.VMEM((2, RING * RING) + piece, BF16),
            pltpu.VMEM((RING, 2) + piece, BF16),
            pltpu.VMEM((RING, 2) + piece, BF16),
            pltpu.VMEM((RING, 2) + piece, BF16),
            pltpu.VMEM((6,) + piece, BF16),
            pltpu.VMEM((2,) + piece, F32),
            pltpu.VMEM((2,) + piece, BF16),
            pltpu.VMEM((2,) + piece, BF16),
            pltpu.VMEM((2,) + piece, BF16),
            pltpu.VMEM((2, 2) + piece, BF16),
            pltpu.VMEM((2, 2) + piece, BF16),
            pltpu.SemaphoreType.DMA((RS_COPIES,)),
            pltpu.SemaphoreType.DMA((RS_COPIES,)),
        ],
        compiler_params=pltpu.CompilerParams(
            collective_id=1, has_side_effects=True, vmem_limit_bytes=VM_K3
        ),
        name="scatter_grads",
    )(rows, tab, in_vmem(x), in_vmem(dy), in_vmem(hid), in_vmem(pgr))


def on_device(tokens, cotangent, up_w, dn_w, block_rows, block_cols, owner_counts):
    devices = lax.axis_size("dp") * lax.axis_size("fsdp")
    scale = 1.0 / math.sqrt(tokens.shape[0] * devices)
    up_full, dn_full, x, dy, tab = gather_weights(
        block_rows, block_cols, owner_counts, up_w, dn_w, tokens, cotangent
    )
    output, input_grad, hid, pgr = local_layer(
        block_rows, block_cols, tab, x, dy, up_full, dn_full
    )
    up_grad, down_grad = scatter_grads(block_rows, tab, x, dy, hid, pgr, scale)
    return output, input_grad, up_grad, down_grad


def solution(mesh):
    in_specs = (
        P(("dp", "fsdp"), None),
        P(("dp", "fsdp"), None),
        P("fsdp", None, None),
        P("fsdp", None, None),
        P(),
        P(),
        P(),
    )
    out_specs = (
        P(("dp", "fsdp"), None),
        P(("dp", "fsdp"), None),
        P("fsdp", None, None),
        P("fsdp", None, None),
    )
    return jax.shard_map(
        on_device, mesh=mesh, in_specs=in_specs, out_specs=out_specs, check_vma=False
    )
```

time: 116 us -> 95 us (0.82); the launches traced: 114 us -> 94.9 us
  Pallas kernels: 110 us -> 90.8 us
    pallas_call x2, Pallas kernels: 70.6 us -> 47.7 us  [the longest x1 31.8 us: gather_weights(): pl.pallas_call(gather_kernel, out_shape=(full, full, cut, cut, jax.ShapeD...]
    pallas_call x1, Pallas kernels: 39.3 us -> 43.1 us  [scatter_grads(): pl.pallas_call(functools.partial(scatter_kernel, scale), out_shape=(grad,...]
    unnamed x4 -> x12, local copies, waits for them, and re-layouts: 3.59 us -> 3.37 us
where the time goes in v2:
time: 95 us; the launch traced here: 94.9 us
  Pallas kernels  90.8 us (96%)
  local copies, waits for them, and re-layouts  3.37 us (4%)
    pallas_call x1, Pallas kernels, scatter_grads(): pl.pallas_call(functools.partial(scatter_kernel, scale), out_shape=(grad,...  43.1 us
    pallas_call x1, Pallas kernels, gather_weights(): pl.pallas_call(gather_kernel, out_shape=(full, full, cut, cut, jax.ShapeD...  31.8 us
    pallas_call x1, Pallas kernels, local_layer(): pl.pallas_call(layer_kernel, out_shape=(result, result, kept, kept), in_s...  15.8 us
    unnamed x12, local copies, waits for them, and re-layouts  3.37 us

profile of v2, /device:TPU:1, one launch (start us, length us, event | category | flops | bytes accessed | tf_op | source)
XLA Modules:
  0.0 94.9 jit_solution(11921791286838510747)
XLA Ops:
  0.6 0.0 copy-start
  0.6 0.6 copy-done
  1.3 0.0 copy-start.2
  1.3 0.7 copy-done.2
  1.9 0.0 copy-start.4
  1.9 0.7 copy-done.4
  2.6 0.0 copy-start.1
  2.6 0.0 copy-start.3
  2.6 31.8 %gather_weights.1 = (bf16[32,4,128,128]{3,2,1,0:T(8,128)(2,1)S(1)}, bf16[32,4,128,128]{3,2,1,0:T(8,128)(2,1)S(1)}, bf16[48,256,128]{2,1,0:T(8,128)(2,1)S(1)}, bf...) custom-call(s32[1,128]{1,0:T(1,128)S(1)} %bitcast.6, s32[1,128]{1,0:T(1,128)S(1)} %bitcast.7, s32[32]{0:T(128)S(1)} %copy-done.4, ...), custom_call_target="tpu_custom_call" | custom-call | tf_op jit(solution)/shard_map/gather_weights/pallas_call | solution.py:264
  34.5 0.0 copy-done.1
  34.5 0.0 copy-done.3
  34.5 15.8 %local_layer.1 = (bf16[256,6144]{1,0:T(8,128)(2,1)}, bf16[256,6144]{1,0:T(8,128)(2,1)}, bf16[130,256,128]{2,1,0:T(8,128)(2,1)S(1)}, bf16[130,256,128]{2,1,0:T(8,128)(2,1)S(1)}) custom-call(s32[128]{0:T(128)S(1)} %copy-done.1, s32[128]{0:T(128)S(1)} %copy-done.3, s32[8,128]{1,0:T(8,128)S(1)} %get-tuple-element.15.tab, ...), custom_call_target="tpu_custom_call" | custom-call | tf_op jit(solution)/shard_map/local_layer/pallas_call | solution.py:378
  50.3 43.1 %scatter_grads.1 = (f32[4,128,128]{2,1,0:T(8,128)S(1)}, f32[4,128,128]{2,1,0:T(8,128)S(1)}) custom-call(s32[128]{0:T(128)S(1)} %copy-done.1, s32[8,128]{1,0:T(8,128)S(1)} %get-tuple-element.15.tab, bf16[48,256,128]{2,1,0:T(8,128)(2,1)S(1)} %get-tuple-element.16.x, bf16[48,256,128]{2,1,0:T(8,128)(2,1)S(1)} %get-tuple-element.17.dy, ...), custom_call_target="tpu_custom_call" | custom-call | tf_op jit(solution)/shard_map/scatter_grads/pallas_call | solution.py:555
  93.5 0.7 copy.13
  94.2 0.7 copy.14
Async XLA Ops:
  0.6 0.7 copy-start
  1.3 0.7 copy-start.2
  1.9 0.7 copy-start.4
  2.6 31.9 %copy-start.1 = (s32[128]{0:T(128)S(1)}, s32[128]{0:T(128)}, u32[]{:S(2)}) copy-start(s32[128]{0:T(128)} %rows.3) | copy-start | bytes 1540
  2.6 31.9 %copy-start.3 = (s32[128]{0:T(128)S(1)}, s32[128]{0:T(128)}, u32[]{:S(2)}) copy-start(s32[128]{0:T(128)} %cols.1) | copy-start | bytes 1540

commit v3 on v2

--- a/solution.py
+++ b/solution.py
@@ -20,12 +20,13 @@
 
 
 def gelu_parts(values):
-    inner_arg = gelu_scale * (values + cubic_coef * values * values * values)
-    tanh_val = jnp.tanh(inner_arg)
-    gelu_value = 0.5 * values * (1.0 + tanh_val)
-    gelu_slope = 0.5 * (1.0 + tanh_val) + 0.5 * values * (
-        1.0 - tanh_val * tanh_val
-    ) * gelu_scale * (1.0 + 3.0 * cubic_coef * values * values)
+    square = values * values
+    tanh_val = jnp.tanh(values * (gelu_scale + gelu_scale * cubic_coef * square))
+    half = 0.5 * values
+    gelu_value = half + half * tanh_val
+    gelu_slope = (0.5 + 0.5 * tanh_val) + half * (1.0 - tanh_val * tanh_val) * (
+        gelu_scale + 3.0 * gelu_scale * cubic_coef * square
+    )
     return gelu_value, gelu_slope
 
 
@@ -47,10 +48,12 @@
         return (self.x * RING + self.y) * 2 + (1 - self.c)
 
 
-def greet(targets):
+def greet(targets, meanwhile=None):
     barrier = pltpu.get_barrier_semaphore()
     for target in targets:
         pl.semaphore_signal(barrier, inc=1, device_id=target, device_id_type=MESH_ID)
+    if meanwhile is not None:
+        meanwhile()
     pl.semaphore_wait(barrier, len(targets))
 
 
@@ -153,8 +156,9 @@
 
 
 def gather_kernel(
-    rows_ref, cols_ref, counts, up_ref, dn_ref, x_hbm, dy_hbm,
-    gu_ref, gd_ref, x_ref, dy_ref, tab_ref, own_sem, send_sem, recv_sem,
+    rows_hbm, cols_hbm, counts_hbm, up_ref, dn_ref, x_hbm, dy_hbm,
+    gu_ref, gd_ref, x_ref, dy_ref, tab_ref, rows_ref, cols_ref, counts,
+    own_sem, send_sem, recv_sem,
 ):
     spot = Spot()
     mine = (up_ref, dn_ref)
@@ -162,7 +166,6 @@
     first_p, first_m = {"fsdp": spot.owner(1, 0)}, {"fsdp": spot.owner(3, 0)}
     second_p, second_m = {"fsdp": spot.owner(0, 1)}, {"fsdp": spot.owner(0, 3)}
     other = {"fsdp": spot.sibling()}
-    greet([first_p, first_m, second_p, second_m, other])
     mail = Mail(send_sem, recv_sem)
     me = spot.owner(0, 0)
 
@@ -185,7 +188,9 @@
     keeps = [
         pltpu.make_async_copy(src, dst, own_sem.at[n])
         for n, (src, dst) in enumerate((
-            (up_ref, gu_ref.at[me]), (dn_ref, gd_ref.at[me])
+            (up_ref, gu_ref.at[me]), (dn_ref, gd_ref.at[me]),
+            (x_ref, x_ref), (dy_ref, dy_ref),
+            (rows_hbm, rows_ref), (cols_hbm, cols_ref), (counts_hbm, counts),
         ))
     ]
     blocks = x_ref.shape[0]
@@ -196,6 +201,12 @@
         pltpu.make_async_copy(dy_hbm.at[:, at], dy_ref.at[b], own_sem.at[3]).start()
         return carry
 
+    def load():
+        for n in (4, 5, 6, 0, 1):
+            keeps[n].start()
+        lax.fori_loop(0, blocks, cut, 0)
+
+    greet([first_p, first_m, second_p, second_m, other], load)
     for h in (0, 1):
         mail.send(mine[h], place(0, 0, h), first_p, ("fst", 3, h))
         mail.send(mine[1 - h], place(0, 0, 1 - h), first_m, ("fst", 1, 1 - h))
@@ -203,9 +214,8 @@
         second(0, h)
     for h in (0, 1):
         share(0, 0, h)
-    for keep in keeps:
-        keep.start()
-    lax.fori_loop(0, blocks, cut, 0)
+    for n in (4, 5, 6):
+        keeps[n].wait()
     slot_tables(rows_ref, cols_ref, counts, tab_ref)
     arrive(3, 0, 0, ("fst", 3, 0), first_m)
     mail.send(held(3, 0, 0), place(3, 0, 0), first_p, ("fst", 2, 0))
@@ -247,10 +257,8 @@
         for j in range(RING):
             for h in (0, 1):
                 mail.wait(full[h].at[spot.owner(i, j, 1 - spot.c)], ("sib", i, j, h), other)
-    for keep in keeps:
-        keep.wait()
-    pltpu.make_async_copy(x_ref, x_ref, own_sem.at[2]).wait()
-    pltpu.make_async_copy(dy_ref, dy_ref, own_sem.at[3]).wait()
+    for n in range(4):
+        keeps[n].wait()
     mail.finish()
     assert len(mail.sent) == len(mail.keys) == AG_COPIES
 
@@ -267,10 +275,13 @@
             full, full, cut, cut,
             jax.ShapeDtypeStruct((8, SLOT_TOTAL), jnp.int32),
         ),
-        in_specs=[vmem_spec] * 2 + [pl.BlockSpec(memory_space=pltpu.SMEM)] + [any_spec] * 4,
+        in_specs=[any_spec] * 7,
         out_specs=(vmem_spec,) * 5,
         scratch_shapes=[
-            pltpu.SemaphoreType.DMA((4,)),
+            pltpu.VMEM((1, SLOT_TOTAL), jnp.int32),
+            pltpu.VMEM((1, SLOT_TOTAL), jnp.int32),
+            pltpu.SMEM(counts.shape, jnp.int32),
+            pltpu.SemaphoreType.DMA((7,)),
             pltpu.SemaphoreType.DMA((AG_COPIES,)),
             pltpu.SemaphoreType.DMA((AG_COPIES,)),
         ],
@@ -278,8 +289,10 @@
             collective_id=0, has_side_effects=True, vmem_limit_bytes=VM_K1
         ),
         name="gather_weights",
-    )(rows.reshape(1, SLOT_TOTAL), cols.reshape(1, SLOT_TOTAL), counts,
-      in_hbm(up), in_hbm(dn), in_hbm(x), in_hbm(dy))
+    )(
+        in_hbm(rows.reshape(1, SLOT_TOTAL)), in_hbm(cols.reshape(1, SLOT_TOTAL)), in_hbm(counts),
+        in_hbm(up), in_hbm(dn), in_hbm(x), in_hbm(dy),
+    )
 
 
 NT = (((1,), (1,)), ((), ()))
@@ -405,13 +418,13 @@
     return pltpu.with_memory_space_constraint(array, pltpu.VMEM)
 
 
-RS_COPIES = 66
+RS_COPIES = 50
 VM_K3 = 26 << 20
 
 
 def scatter_kernel(
     scale, rows, tab, x, dy, hid, pgr, ug_ref, dg_ref,
-    stage, own, sib, mid, got_m, got_p, r_bf, r_f32, mid2, fin_m, fin_p, zsend, zrecv,
+    stage, own, sib, mid, got_m, got_p, r_own, r_bf, r_f32, mid2, fin_m, fin_p, zsend, zrecv,
     send_sem, recv_sem,
 ):
     spot = Spot()
@@ -421,7 +434,6 @@
     other = {"fsdp": spot.sibling()}
     z_a = {"dp": spot.z + 1 - 2 * lax.rem(spot.z, 2)}
     z_b = {"dp": RING - 1 - spot.z}
-    greet([first_p, first_m, second_p, second_m, other, z_a, z_b])
     mail = Mail(send_sem, recv_sem)
 
     def partial(owner, h, q):
@@ -430,95 +442,99 @@
             return mm(x[rows[k]], pgr[tab[LAST, k]], TN)
         return mm(hid[tab[LAST, k]], dy[rows[k]], TN)
 
-    def give(j):
-        def step(n, carry):
-            i = turn(n)
-            at = i * RING + j
-            for h in (0, 1):
-                for q in range(SLOTS):
-                    stage[h, at, q] = partial(spot.owner(i, j, 1 - spot.c), h, q).astype(BF16)
-                mail.send_at(stage.at[h, at], sib.at[h, at], other, 2 * at + h)
-            return carry
-        lax.fori_loop(0, RING, step, 0)
-
-    def pair(i, j, h, then, *more):
+    def make(i, j):
         at = i * RING + j
-        mail.wait_at(sib.at[h, at], other, 2 * at + h)
+        for h in (0, 1):
+            for q in range(SLOTS):
+                stage[at, h, q] = partial(spot.owner(i, j, 1 - spot.c), h, q).astype(BF16)
+
+    def give(i, j):
+        at = i * RING + j
+        mail.send_at(stage.at[at], sib.at[at], other, at)
+
+    def given(i, j):
+        at = i * RING + j
+        mail.wait_at(sib.at[at], other, at)
+
+    def keep(i, j, h, *more):
+        at = i * RING + j
         for q in range(SLOTS):
-            value = partial(spot.owner(i, j), h, q) + sib[h, at, q].astype(F32)
+            value = partial(spot.owner(i, j), h, q) + sib[at, h, q].astype(F32)
             for ref in more:
                 value = value + ref[q].astype(F32)
-            then(q, value)
-
-    def keep(i, j, h, *more):
-        at = i * RING + j
-
-        def then(q, value):
-            own[h, at, q] = value.astype(BF16)
-
-        pair(i, j, h, then, *more)
-        return own.at[h, at]
-
-    base = 2 * RING * RING
-    give(2)
-    give(3)
-
-    def far(n, carry):
-        i = turn(n)
-        mail.send_at(keep(i, 2, 0), mid.at[i, 0], second_p, base + i)
-        mail.send_at(keep(i, 2, 1), mid.at[i, 1], second_m, base + RING + i)
-        return carry
-
-    lax.fori_loop(0, RING, far, 0)
-    give(1)
-    base += 2 * RING
-
-    def near(n, carry):
-        i = turn(n)
+            own[at, h, q] = value.astype(BF16)
+        return own.at[at, h]
+
+    mids = RING * RING
+    base = mids + 2 * RING
+    one = base + 4 * RING
+
+    def turns(*acts):
+        def step(n, carry):
+            for act in acts:
+                act(turn(n))
+            return carry
+        return step
+
+    def make_give(j):
+        def act(i):
+            make(i, j)
+            give(i, j)
+        return act
+
+    def far(i):
+        given(i, 2)
+        mail.send_at(keep(i, 2, 0), mid.at[i, 0], second_p, mids + i)
+        mail.send_at(keep(i, 2, 1), mid.at[i, 1], second_m, mids + RING + i)
+
+    def near(i):
+        given(i, 1)
         mail.send_at(keep(i, 1, 1), got_m.at[i, 1], second_p, base + i)
+        given(i, 3)
         mail.send_at(keep(i, 3, 0), got_p.at[i, 0], second_m, base + RING + i)
-        mail.wait_at(mid.at[i, 0], second_m, base - 2 * RING + i)
+        mail.wait_at(mid.at[i, 0], second_m, mids + i)
         mail.send_at(keep(i, 1, 0, mid.at[i, 0]), got_m.at[i, 0], second_p, base + 2 * RING + i)
-        mail.wait_at(mid.at[i, 1], second_p, base - RING + i)
+        mail.wait_at(mid.at[i, 1], second_p, mids + RING + i)
         mail.send_at(keep(i, 3, 1, mid.at[i, 1]), got_p.at[i, 1], second_m, base + 3 * RING + i)
-        return carry
-
-    lax.fori_loop(0, RING, near, 0)
-    give(0)
-
-    def ring_sum(i, h, then):
+
+    def stay(i):
+        given(i, 0)
+        at = i * RING
+        for h in (0, 1):
+            for q in range(SLOTS):
+                r_own[i, h, q] = partial(spot.owner(i, 0), h, q) + sib[at, h, q].astype(F32)
+
+    def ring_sum(i, h):
         mail.wait_at(got_m.at[i, h], second_m, base + (2 * RING, 0)[h] + i)
         mail.wait_at(got_p.at[i, h], second_p, base + (RING, 3 * RING)[h] + i)
-        pair(i, 0, h, then, got_m.at[i, h], got_p.at[i, h])
-
-    one = base + 4 * RING
-    for n, (i, h, dst, target) in enumerate((
-        (2, 0, mid2.at[0], first_p),
-        (2, 1, mid2.at[1], first_m),
-        (1, 1, fin_m.at[1], first_p),
-        (3, 0, fin_p.at[0], first_m),
-    )):
-        def store(q, value):
-            r_bf[n, q] = value.astype(BF16)
-
-        ring_sum(i, h, store)
-        mail.send_at(r_bf.at[n], dst, target, one + n)
-    for n, (i, h, dst, target, source) in enumerate((
-        (1, 0, fin_m.at[0], first_p, first_m),
-        (3, 1, fin_p.at[1], first_m, first_p),
-    )):
-        def store(q, value):
-            r_f32[n, q] = value
-
-        ring_sum(i, h, store)
-        mail.wait_at(mid2.at[h], source, one + h)
-        r_bf[4 + n] = (r_f32[n] + mid2[h].astype(F32)).astype(BF16)
-        mail.send_at(r_bf.at[4 + n], dst, target, one + 4 + n)
+        return r_own[i, h] + got_m[i, h].astype(F32) + got_p[i, h].astype(F32)
+
+    def pass_on(n, i, h, dst, target):
+        r_bf[n] = ring_sum(i, h).astype(BF16)
+        mail.send_at(r_bf.at[n], dst.at[h], target, one + n)
+
+    def add_on(n, i, h, dst, target):
+        value = ring_sum(i, h)
+        mail.wait_at(mid2.at[h], (first_m, first_p)[h], one + h)
+        r_bf[4 + n] = (value + mid2[h].astype(F32)).astype(BF16)
+        mail.send_at(r_bf.at[4 + n], dst.at[h], target, one + 4 + n)
+
+    greet(
+        [first_p, first_m, second_p, second_m, other, z_a, z_b],
+        lambda: lax.fori_loop(0, RING, turns(lambda i: make(i, 2)), 0),
+    )
+    lax.fori_loop(0, 4, turns(lambda i: give(i, 2)), 0)
+    lax.fori_loop(0, 4, turns(far, make_give(3), make_give(1)), 0)
+    lax.fori_loop(0, 4, turns(near, make_give(0)), 0)
+    lax.fori_loop(0, 4, turns(stay), 0)
+    pass_on(0, 2, 0, mid2, first_p)
+    pass_on(1, 2, 1, mid2, first_m)
+    pass_on(2, 1, 1, fin_m, first_p)
+    pass_on(3, 3, 0, fin_p, first_m)
+    add_on(0, 1, 0, fin_m, first_p)
+    add_on(1, 3, 1, fin_p, first_m)
     for h in (0, 1):
-        def store(q, value):
-            r_f32[h, q] = value
-
-        ring_sum(0, h, store)
+        r_f32[h] = ring_sum(0, h)
     plane = one + 6
     for h in (0, 1):
         mail.wait_at(fin_m.at[h], first_m, one + (4, 2)[h])
@@ -537,10 +553,15 @@
         final[h][...] = value * scale
 
     def sent(n, carry):
-        mail.sent_at(stage.at[0, 0], other, n)
+        mail.sent_at(mid.at[0, 0], other, n)
         return carry
 
-    lax.fori_loop(0, RS_COPIES, sent, 0)
+    def sent_pair(n, carry):
+        mail.sent_at(stage.at[0], other, n)
+        return carry
+
+    lax.fori_loop(0, mids, sent_pair, 0)
+    lax.fori_loop(mids, RS_COPIES, sent, 0)
 
 
 def turn(n):
@@ -558,12 +579,13 @@
         in_specs=[smem] * 2 + [vmem] * 4,
         out_specs=(vmem, vmem),
         scratch_shapes=[
-            pltpu.VMEM((2, RING * RING) + piece, BF16),
-            pltpu.VMEM((2, RING * RING) + piece, BF16),
-            pltpu.VMEM((2, RING * RING) + piece, BF16),
+            pltpu.VMEM((RING * RING, 2) + piece, BF16),
+            pltpu.VMEM((RING * RING, 2) + piece, BF16),
+            pltpu.VMEM((RING * RING, 2) + piece, BF16),
             pltpu.VMEM((RING, 2) + piece, BF16),
             pltpu.VMEM((RING, 2) + piece, BF16),
             pltpu.VMEM((RING, 2) + piece, BF16),
+            pltpu.VMEM((RING, 2) + piece, F32),
             pltpu.VMEM((6,) + piece, BF16),
             pltpu.VMEM((2,) + piece, F32),
             pltpu.VMEM((2,) + piece, BF16),

time: 95 us -> 89.4 us (0.941)
  Pallas kernels: 90.8 us -> 87.2 us
  local copies, waits for them, and re-layouts: 3.37 us -> 1.42 us
    pallas_call x1, Pallas kernels: 43.1 us -> 39.4 us  [scatter_grads(): pl.pallas_call(functools.partial(scatter_kernel, scale), out_shape=(grad,...]
    unnamed x12 -> x6, local copies, waits for them, and re-layouts: 3.37 us -> 1.42 us
where the time goes in v3:
time: 89.4 us; the launch traced here: 89.3 us
  Pallas kernels  87.2 us (98%)
  local copies, waits for them, and re-layouts  1.42 us (2%)
    pallas_call x1, Pallas kernels, scatter_grads(): pl.pallas_call(functools.partial(scatter_kernel, scale), out_shape=(grad,...  39.4 us
    pallas_call x1, Pallas kernels, gather_weights(): pl.pallas_call(gather_kernel, out_shape=(full, full, cut, cut, jax.ShapeD...  31.4 us
    pallas_call x1, Pallas kernels, local_layer(): pl.pallas_call(layer_kernel, out_shape=(result, result, kept, kept), in_s...  16.4 us

profile of v3, /device:TPU:1, one launch (start us, length us, event | category | flops | bytes accessed | tf_op | source)
XLA Modules:
  0.0 89.3 jit_solution(12086822479378575162)
XLA Ops:
  0.6 0.0 copy-start
  0.6 0.0 copy-start.1
  0.7 31.4 %gather_weights.1 = (bf16[32,4,128,128]{3,2,1,0:T(8,128)(2,1)S(1)}, bf16[32,4,128,128]{3,2,1,0:T(8,128)(2,1)S(1)}, bf16[48,256,128]{2,1,0:T(8,128)(2,1)S(1)}, bf...) custom-call(s32[1,128]{1,0:T(1,128)} %bitcast.6, s32[1,128]{1,0:T(1,128)} %bitcast.7, s32[32]{0:T(128)} %counts_hbm.1, ...), custom_call_target="tpu_custom_call" | custom-call | tf_op jit(solution)/shard_map/gather_weights/pallas_call | solution.py:272
  32.1 0.0 copy-done
  32.1 0.0 copy-done.1
  32.1 16.4 %local_layer.1 = (bf16[256,6144]{1,0:T(8,128)(2,1)}, bf16[256,6144]{1,0:T(8,128)(2,1)}, bf16[130,256,128]{2,1,0:T(8,128)(2,1)S(1)}, bf16[130,256,128]{2,1,0:T(8,128)(2,1)S(1)}) custom-call(s32[128]{0:T(128)S(1)} %copy-done, s32[128]{0:T(128)S(1)} %copy-done.1, s32[8,128]{1,0:T(8,128)S(1)} %get-tuple-element.15.tab, ...), custom_call_target="tpu_custom_call" | custom-call | tf_op jit(solution)/shard_map/local_layer/pallas_call | solution.py:391
  48.5 39.4 %scatter_grads.1 = (f32[4,128,128]{2,1,0:T(8,128)S(1)}, f32[4,128,128]{2,1,0:T(8,128)S(1)}) custom-call(s32[128]{0:T(128)S(1)} %copy-done, s32[8,128]{1,0:T(8,128)S(1)} %get-tuple-element.15.tab, bf16[48,256,128]{2,1,0:T(8,128)(2,1)S(1)} %get-tuple-element.16.x, bf16[48,256,128]{2,1,0:T(8,128)(2,1)S(1)} %get-tuple-element.17.dy, ...), custom_call_target="tpu_custom_call" | custom-call | tf_op jit(solution)/shard_map/scatter_grads/pallas_call | solution.py:576
  87.9 0.7 copy.13
  88.6 0.7 copy.14
Async XLA Ops:
  0.6 31.4 %copy-start = (s32[128]{0:T(128)S(1)}, s32[128]{0:T(128)}, u32[]{:S(2)}) copy-start(s32[128]{0:T(128)} %rows.3) | copy-start | bytes 1540
  0.6 31.4 %copy-start.1 = (s32[128]{0:T(128)S(1)}, s32[128]{0:T(128)}, u32[]{:S(2)}) copy-start(s32[128]{0:T(128)} %cols.1) | copy-start | bytes 1540

commit v4 on v3

--- a/solution.py
+++ b/solution.py
@@ -60,59 +60,40 @@
 class Mail:
     def __init__(self, send_sem, recv_sem):
         self.send_sem, self.recv_sem = send_sem, recv_sem
-        self.keys, self.sent = {}, []
-
-    def slot(self, key):
-        return self.keys.setdefault(key, len(self.keys))
-
-    def send(self, src, dst, target, key):
-        copy = pltpu.make_async_remote_copy(
-            src_ref=src,
-            dst_ref=dst,
-            send_sem=self.send_sem.at[len(self.sent)],
-            recv_sem=self.recv_sem.at[self.slot(key)],
-            device_id=target,
-            device_id_type=MESH_ID,
-        )
-        copy.start()
-        self.sent.append(copy)
-
-    def wait(self, dst, key, target):
-        pltpu.make_async_remote_copy(
-            src_ref=dst,
-            dst_ref=dst,
-            send_sem=self.send_sem.at[0],
-            recv_sem=self.recv_sem.at[self.slot(key)],
-            device_id=target,
-            device_id_type=MESH_ID,
-        ).wait_recv()
-
-    def finish(self):
-        for copy in self.sent:
-            copy.wait_send()
-
-    def copy_at(self, src, dst, target, n):
+        self.keys, self.sent = {}, 0
+
+    def copy(self, src, dst, target, n, lane):
         return pltpu.make_async_remote_copy(
             src_ref=src,
             dst_ref=dst,
-            send_sem=self.send_sem.at[n],
+            send_sem=self.send_sem.at[lane],
             recv_sem=self.recv_sem.at[n],
             device_id=target,
             device_id_type=MESH_ID,
         )
 
-    def send_at(self, src, dst, target, n):
-        self.copy_at(src, dst, target, n).start()
+    def slot(self, key):
+        return key if isinstance(key, int) else self.keys.setdefault(key, 2 + len(self.keys))
+
+    def send(self, src, dst, target, key, lane=0):
+        self.copy(src, dst, target, self.slot(key), lane).start()
+        self.sent += 1
+
+    def wait(self, dst, key, target):
+        self.copy(dst, dst, target, self.slot(key), 0).wait_recv()
+
+    def send_at(self, src, dst, target, n, lane):
+        self.copy(src, dst, target, n, lane).start()
 
     def wait_at(self, dst, target, n):
-        self.copy_at(dst, dst, target, n).wait_recv()
-
-    def sent_at(self, src, target, n):
-        self.copy_at(src, src, target, n).wait_send()
+        self.copy(dst, dst, target, n, 0).wait_recv()
+
+    def sent_all(self, like, target, lane):
+        self.copy(like, like, target, 0, lane).wait_send()
 
 
 VM_K1 = 8 << 20
-AG_COPIES = 62
+RING_COPIES = 30
 SLOT_TOTAL = 128
 DEAD = SLOT_TOTAL
 BY_COL, BY_ROW, LAST, LIVE = 0, 1, 2, 3
@@ -179,7 +160,7 @@
         mail.wait(place(i, j, h), key, source)
 
     def share(i, j, h):
-        mail.send(held(i, j, h), place(i, j, h), other, ("sib", i, j, h))
+        mail.send(held(i, j, h), place(i, j, h), other, h, lane=1)
 
     def second(i, h):
         mail.send(held(i, 0, h), place(i, 0, h), second_p, ("sec", i, 3, h))
@@ -253,14 +234,13 @@
         share(i, 2, 0)
         arrive(i, 2, 1, ("sec", i, 2, 1), second_p)
         share(i, 2, 1)
-    for i in range(RING):
-        for j in range(RING):
-            for h in (0, 1):
-                mail.wait(full[h].at[spot.owner(i, j, 1 - spot.c)], ("sib", i, j, h), other)
+    for h in (0, 1):
+        mail.wait(full[h].at[pl.ds(0, RING * RING)], h, other)
     for n in range(4):
         keeps[n].wait()
-    mail.finish()
-    assert len(mail.sent) == len(mail.keys) == AG_COPIES
+    mail.sent_all(gu_ref.at[pl.ds(0, RING_COPIES)], other, 0)
+    mail.sent_all(gu_ref, other, 1)
+    assert len(mail.keys) == RING_COPIES and mail.sent == RING_COPIES + gu_ref.shape[0]
 
 
 def gather_weights(rows, cols, counts, up, dn, x, dy):
@@ -282,8 +262,8 @@
             pltpu.VMEM((1, SLOT_TOTAL), jnp.int32),
             pltpu.SMEM(counts.shape, jnp.int32),
             pltpu.SemaphoreType.DMA((7,)),
-            pltpu.SemaphoreType.DMA((AG_COPIES,)),
-            pltpu.SemaphoreType.DMA((AG_COPIES,)),
+            pltpu.SemaphoreType.DMA((2,)),
+            pltpu.SemaphoreType.DMA((2 + RING_COPIES,)),
         ],
         compiler_params=pltpu.CompilerParams(
             collective_id=0, has_side_effects=True, vmem_limit_bytes=VM_K1
@@ -304,7 +284,7 @@
     return lax.dot_general(a, b, dims, preferred_element_type=F32)
 
 
-UNROLL = 4
+UNROLL, REST = 10, 2
 
 
 def layer_kernel(
@@ -313,7 +293,8 @@
     row_blocks, tok = x.shape[:2]
     width = row_blocks * EDGE
     n_live = tab[LIVE, 0]
-    steps = (n_live + UNROLL - 1) // UNROLL
+    whole = n_live // UNROLL
+    rest = (n_live - whole * UNROLL + REST - 1) // REST
 
     def block(b):
         return pl.ds(pl.multiple_of(b * EDGE, EDGE), EDGE)
@@ -321,10 +302,10 @@
     hid[DEAD] = jnp.zeros((tok, EDGE), BF16)
     pgr[DEAD] = jnp.zeros((tok, EDGE), BF16)
 
-    def forward(step, carry):
+    def forward(width, start, step, carry):
         pre, back = acc[0], acc[1]
-        for u in range(UNROLL):
-            s = step * UNROLL + u
+        for u in range(width):
+            s = start + step * width + u
             k = tab[BY_COL, jnp.minimum(s, n_live - 1)]
             before = tab[BY_COL, jnp.clip(s - 1, 0, n_live - 1)]
             r = rows[k]
@@ -339,7 +320,8 @@
         acc[1] = back
         return carry
 
-    lax.fori_loop(0, steps, forward, 0)
+    lax.fori_loop(0, whole, functools.partial(forward, UNROLL, 0), 0)
+    lax.fori_loop(0, rest, functools.partial(forward, REST, whole * UNROLL), 0)
 
     def clear(b, carry):
         out[:, block(b)] = jnp.zeros((tok, EDGE), BF16)
@@ -353,10 +335,10 @@
         pltpu.make_async_copy(inp.at[:, block(b)], in_hbm.at[:, block(b)], sem.at[1]).start()
         return carry
 
-    def backward(step, done):
+    def backward(width, start, step, done):
         o, g = acc[0], acc[1]
-        for u in range(UNROLL):
-            t = step * UNROLL + u
+        for u in range(width):
+            t = start + step * width + u
             k = tab[BY_ROW, jnp.minimum(t, n_live - 1)]
             r = rows[k]
             before = tab[BY_ROW, jnp.clip(t - 1, 0, n_live - 1)]
@@ -369,15 +351,16 @@
             inp[:, to] = g.astype(BF16)
         acc[0] = o
         acc[1] = g
-        upto = rows[tab[BY_ROW, jnp.minimum((step + 1) * UNROLL - 1, n_live - 1)]]
+        upto = rows[tab[BY_ROW, jnp.minimum(start + (step + 1) * width - 1, n_live - 1)]]
         lax.fori_loop(done, upto, put, 0)
         return upto
 
-    done = lax.fori_loop(0, steps, backward, 0)
+    done = lax.fori_loop(0, whole, functools.partial(backward, UNROLL, 0), 0)
+    done = lax.fori_loop(0, rest, functools.partial(backward, REST, whole * UNROLL), done)
     lax.fori_loop(done, row_blocks, put, 0)
-    whole = pl.ds(0, width)
-    pltpu.make_async_copy(out.at[:, whole], out_hbm, sem.at[0]).wait()
-    pltpu.make_async_copy(inp.at[:, whole], in_hbm, sem.at[1]).wait()
+    every = pl.ds(0, width)
+    pltpu.make_async_copy(out.at[:, every], out_hbm, sem.at[0]).wait()
+    pltpu.make_async_copy(inp.at[:, every], in_hbm, sem.at[1]).wait()
 
 
 def local_layer(rows, cols, tab, x, dy, up, dn):
@@ -418,7 +401,8 @@
     return pltpu.with_memory_space_constraint(array, pltpu.VMEM)
 
 
-RS_COPIES = 50
+TAIL = 4
+RS_COPIES = 40 + 10 * TAIL
 VM_K3 = 26 << 20
 
 
@@ -450,7 +434,7 @@
 
     def give(i, j):
         at = i * RING + j
-        mail.send_at(stage.at[at], sib.at[at], other, at)
+        mail.send_at(stage.at[at], sib.at[at], other, at, 0)
 
     def given(i, j):
         at = i * RING + j
@@ -465,6 +449,7 @@
             own[at, h, q] = value.astype(BF16)
         return own.at[at, h]
 
+    shares = [pl.ds(p * SLOTS // TAIL, SLOTS // TAIL) for p in range(TAIL)]
     mids = RING * RING
     base = mids + 2 * RING
     one = base + 4 * RING
@@ -484,18 +469,18 @@
 
     def far(i):
         given(i, 2)
-        mail.send_at(keep(i, 2, 0), mid.at[i, 0], second_p, mids + i)
-        mail.send_at(keep(i, 2, 1), mid.at[i, 1], second_m, mids + RING + i)
+        mail.send_at(keep(i, 2, 0), mid.at[i, 0], second_p, mids + i, 1)
+        mail.send_at(keep(i, 2, 1), mid.at[i, 1], second_m, mids + RING + i, 1)
 
     def near(i):
         given(i, 1)
-        mail.send_at(keep(i, 1, 1), got_m.at[i, 1], second_p, base + i)
+        mail.send_at(keep(i, 1, 1), got_m.at[i, 1], second_p, base + i, 1)
         given(i, 3)
-        mail.send_at(keep(i, 3, 0), got_p.at[i, 0], second_m, base + RING + i)
+        mail.send_at(keep(i, 3, 0), got_p.at[i, 0], second_m, base + RING + i, 1)
         mail.wait_at(mid.at[i, 0], second_m, mids + i)
-        mail.send_at(keep(i, 1, 0, mid.at[i, 0]), got_m.at[i, 0], second_p, base + 2 * RING + i)
+        mail.send_at(keep(i, 1, 0, mid.at[i, 0]), got_m.at[i, 0], second_p, base + 2 * RING + i, 1)
         mail.wait_at(mid.at[i, 1], second_p, mids + RING + i)
-        mail.send_at(keep(i, 3, 1, mid.at[i, 1]), got_p.at[i, 1], second_m, base + 3 * RING + i)
+        mail.send_at(keep(i, 3, 1, mid.at[i, 1]), got_p.at[i, 1], second_m, base + 3 * RING + i, 1)
 
     def stay(i):
         given(i, 0)
@@ -504,20 +489,24 @@
             for q in range(SLOTS):
                 r_own[i, h, q] = partial(spot.owner(i, 0), h, q) + sib[at, h, q].astype(F32)
 
-    def ring_sum(i, h):
+    def rung(i, h):
         mail.wait_at(got_m.at[i, h], second_m, base + (2 * RING, 0)[h] + i)
         mail.wait_at(got_p.at[i, h], second_p, base + (RING, 3 * RING)[h] + i)
-        return r_own[i, h] + got_m[i, h].astype(F32) + got_p[i, h].astype(F32)
+
+    def ring_sum(i, h, of):
+        return r_own[i, h, of] + got_m[i, h, of].astype(F32) + got_p[i, h, of].astype(F32)
 
     def pass_on(n, i, h, dst, target):
-        r_bf[n] = ring_sum(i, h).astype(BF16)
-        mail.send_at(r_bf.at[n], dst.at[h], target, one + n)
-
-    def add_on(n, i, h, dst, target):
-        value = ring_sum(i, h)
-        mail.wait_at(mid2.at[h], (first_m, first_p)[h], one + h)
-        r_bf[4 + n] = (value + mid2[h].astype(F32)).astype(BF16)
-        mail.send_at(r_bf.at[4 + n], dst.at[h], target, one + 4 + n)
+        rung(i, h)
+        for p, of in enumerate(shares):
+            r_bf[n, of] = ring_sum(i, h, of).astype(BF16)
+            mail.send_at(r_bf.at[n, of], dst.at[h, of], target, one + 6 * p + n, 2)
+
+    def add_on(p, of, n, i, h, dst, target):
+        value = ring_sum(i, h, of)
+        mail.wait_at(mid2.at[h, of], (first_m, first_p)[h], one + 6 * p + h)
+        r_bf[4 + n, of] = (value + mid2[h, of].astype(F32)).astype(BF16)
+        mail.send_at(r_bf.at[4 + n, of], dst.at[h, of], target, one + 6 * p + 4 + n, 2)
 
     greet(
         [first_p, first_m, second_p, second_m, other, z_a, z_b],
@@ -531,37 +520,41 @@
     pass_on(1, 2, 1, mid2, first_m)
     pass_on(2, 1, 1, fin_m, first_p)
     pass_on(3, 3, 0, fin_p, first_m)
-    add_on(0, 1, 0, fin_m, first_p)
-    add_on(1, 3, 1, fin_p, first_m)
+    rung(1, 0)
+    rung(3, 1)
+    for p, of in enumerate(shares):
+        add_on(p, of, 0, 1, 0, fin_m, first_p)
+        add_on(p, of, 1, 3, 1, fin_p, first_m)
     for h in (0, 1):
-        r_f32[h] = ring_sum(0, h)
-    plane = one + 6
-    for h in (0, 1):
-        mail.wait_at(fin_m.at[h], first_m, one + (4, 2)[h])
-        mail.wait_at(fin_p.at[h], first_p, one + (3, 5)[h])
-        value = r_f32[h] + fin_m[h].astype(F32) + fin_p[h].astype(F32)
-        zsend[0, h] = value.astype(BF16)
-        mail.send_at(zsend.at[0, h], zrecv.at[0, h], (z_a, z_b)[h], plane + h)
-    for h in (0, 1):
-        mail.wait_at(zrecv.at[0, h], (z_a, z_b)[h], plane + h)
-        value = zsend[0, h].astype(F32) + zrecv[0, h].astype(F32)
-        zsend[1, h] = value.astype(BF16)
-        mail.send_at(zsend.at[1, h], zrecv.at[1, h], (z_b, z_a)[h], plane + 2 + h)
-    for h in (0, 1):
-        mail.wait_at(zrecv.at[1, h], (z_b, z_a)[h], plane + 2 + h)
-        value = zsend[1, h].astype(F32) + zrecv[1, h].astype(F32)
-        final[h][...] = value * scale
-
-    def sent(n, carry):
-        mail.sent_at(mid.at[0, 0], other, n)
-        return carry
-
-    def sent_pair(n, carry):
-        mail.sent_at(stage.at[0], other, n)
-        return carry
-
-    lax.fori_loop(0, mids, sent_pair, 0)
-    lax.fori_loop(mids, RS_COPIES, sent, 0)
+        rung(0, h)
+        r_f32[h] = ring_sum(0, h, slice(None))
+    plane = one + 6 * TAIL
+    for p, of in enumerate(shares):
+        for h in (0, 1):
+            mail.wait_at(fin_m.at[h, of], first_m, one + 6 * p + (4, 2)[h])
+            mail.wait_at(fin_p.at[h, of], first_p, one + 6 * p + (3, 5)[h])
+            value = r_f32[h, of] + fin_m[h, of].astype(F32) + fin_p[h, of].astype(F32)
+            zsend[0, h, of] = value.astype(BF16)
+            mail.send_at(
+                zsend.at[0, h, of], zrecv.at[0, h, of], (z_a, z_b)[h], plane + 4 * p + h, 2
+            )
+    for p, of in enumerate(shares):
+        for h in (0, 1):
+            mail.wait_at(zrecv.at[0, h, of], (z_a, z_b)[h], plane + 4 * p + h)
+            value = zsend[0, h, of].astype(F32) + zrecv[0, h, of].astype(F32)
+            zsend[1, h, of] = value.astype(BF16)
+            mail.send_at(
+                zsend.at[1, h, of], zrecv.at[1, h, of], (z_b, z_a)[h], plane + 4 * p + 2 + h, 2
+            )
+    for p, of in enumerate(shares):
+        for h in (0, 1):
+            mail.wait_at(zrecv.at[1, h, of], (z_b, z_a)[h], plane + 4 * p + 2 + h)
+            value = zsend[1, h, of].astype(F32) + zrecv[1, h, of].astype(F32)
+            final[h][of] = value * scale
+
+    mail.sent_all(stage, other, 0)
+    mail.sent_all(own.at[pl.ds(0, 3 * RING)], other, 1)
+    mail.sent_all(own.at[pl.ds(0, 5)], other, 2)
 
 
 def turn(n):
@@ -593,7 +586,7 @@
             pltpu.VMEM((2,) + piece, BF16),
             pltpu.VMEM((2, 2) + piece, BF16),
             pltpu.VMEM((2, 2) + piece, BF16),
-            pltpu.SemaphoreType.DMA((RS_COPIES,)),
+            pltpu.SemaphoreType.DMA((3,)),
             pltpu.SemaphoreType.DMA((RS_COPIES,)),
         ],
         compiler_params=pltpu.CompilerParams(

time: 89.4 us -> 82.9 us (0.927)
  Pallas kernels: 87.2 us -> 80.7 us
    pallas_call x1, Pallas kernels: 16.4 us -> 12.7 us  [local_layer(): pl.pallas_call(layer_kernel, out_shape=(result, result, kept, kept), in_s...]
    pallas_call x1, Pallas kernels: 39.4 us -> 37.5 us  [scatter_grads(): pl.pallas_call(functools.partial(scatter_kernel, scale), out_shape=(grad,...]
    pallas_call x1, Pallas kernels: 31.4 us -> 30.5 us  [gather_weights(): pl.pallas_call(gather_kernel, out_shape=(full, full, cut, cut, jax.ShapeD...]
where the time goes in v4:
time: 82.9 us; the launch traced here: 82.8 us
  Pallas kernels  80.7 us (97%)
  local copies, waits for them, and re-layouts  1.42 us (2%)
    pallas_call x1, Pallas kernels, scatter_grads(): pl.pallas_call(functools.partial(scatter_kernel, scale), out_shape=(grad,...  37.5 us
    pallas_call x1, Pallas kernels, gather_weights(): pl.pallas_call(gather_kernel, out_shape=(full, full, cut, cut, jax.ShapeD...  30.5 us
    pallas_call x1, Pallas kernels, local_layer(): pl.pallas_call(layer_kernel, out_shape=(result, result, kept, kept), in_s...  12.7 us

profile of v4, /device:TPU:1, one launch (start us, length us, event | category | flops | bytes accessed | tf_op | source)
XLA Modules:
  0.0 82.8 jit_solution(17230016659465711263)
XLA Ops:
  0.6 0.0 copy-start
  0.6 0.0 copy-start.1
  0.7 30.5 %gather_weights.1 = (bf16[32,4,128,128]{3,2,1,0:T(8,128)(2,1)S(1)}, bf16[32,4,128,128]{3,2,1,0:T(8,128)(2,1)S(1)}, bf16[48,256,128]{2,1,0:T(8,128)(2,1)S(1)}, bf...) custom-call(s32[1,128]{1,0:T(1,128)} %bitcast.6, s32[1,128]{1,0:T(1,128)} %bitcast.7, s32[32]{0:T(128)} %counts_hbm.1, ...), custom_call_target="tpu_custom_call" | custom-call | tf_op jit(solution)/shard_map/gather_weights/pallas_call | solution.py:252
  31.2 0.0 copy-done
  31.2 0.0 copy-done.1
  31.2 12.7 %local_layer.1 = (bf16[256,6144]{1,0:T(8,128)(2,1)}, bf16[256,6144]{1,0:T(8,128)(2,1)}, bf16[130,256,128]{2,1,0:T(8,128)(2,1)S(1)}, bf16[130,256,128]{2,1,0:T(8,128)(2,1)S(1)}) custom-call(s32[128]{0:T(128)S(1)} %copy-done, s32[128]{0:T(128)S(1)} %copy-done.1, s32[8,128]{1,0:T(8,128)S(1)} %get-tuple-element.15.tab, ...), custom_call_target="tpu_custom_call" | custom-call | tf_op jit(solution)/shard_map/local_layer/pallas_call | solution.py:374
  43.9 37.5 %scatter_grads.1 = (f32[4,128,128]{2,1,0:T(8,128)S(1)}, f32[4,128,128]{2,1,0:T(8,128)S(1)}) custom-call(s32[128]{0:T(128)S(1)} %copy-done, s32[8,128]{1,0:T(8,128)S(1)} %get-tuple-element.15.tab, bf16[48,256,128]{2,1,0:T(8,128)(2,1)S(1)} %get-tuple-element.16.x, bf16[48,256,128]{2,1,0:T(8,128)(2,1)S(1)} %get-tuple-element.17.dy, ...), custom_call_target="tpu_custom_call" | custom-call | tf_op jit(solution)/shard_map/scatter_grads/pallas_call | solution.py:569
  81.4 0.7 copy.13
  82.1 0.7 copy.14
Async XLA Ops:
  0.6 30.5 %copy-start = (s32[128]{0:T(128)S(1)}, s32[128]{0:T(128)}, u32[]{:S(2)}) copy-start(s32[128]{0:T(128)} %rows.3) | copy-start | bytes 1540
  0.6 30.5 %copy-start.1 = (s32[128]{0:T(128)S(1)}, s32[128]{0:T(128)}, u32[]{:S(2)}) copy-start(s32[128]{0:T(128)} %cols.1) | copy-start | bytes 1540

commit v5 on v4

--- a/solution.py
+++ b/solution.py
@@ -23,9 +23,10 @@
     square = values * values
     tanh_val = jnp.tanh(values * (gelu_scale + gelu_scale * cubic_coef * square))
     half = 0.5 * values
-    gelu_value = half + half * tanh_val
-    gelu_slope = (0.5 + 0.5 * tanh_val) + half * (1.0 - tanh_val * tanh_val) * (
-        gelu_scale + 3.0 * gelu_scale * cubic_coef * square
+    above, below = 1.0 + tanh_val, 1.0 - tanh_val
+    gelu_value = half * above
+    gelu_slope = above * (
+        0.5 + half * below * (gelu_scale + 3.0 * gelu_scale * cubic_coef * square)
     )
     return gelu_value, gelu_slope
 

time: 82.9 us -> 84.1 us (1.014)
  Pallas kernels: 80.7 us -> 81.9 us
    pallas_call x1, Pallas kernels: 12.7 us -> 13.9 us  [local_layer(): pl.pallas_call(layer_kernel, out_shape=(result, result, kept, kept), in_s...]
where the time goes in v5:
time: 84.1 us; the launch traced here: 84 us
  Pallas kernels  81.9 us (97%)
  local copies, waits for them, and re-layouts  1.42 us (2%)
    pallas_call x1, Pallas kernels, scatter_grads(): pl.pallas_call(functools.partial(scatter_kernel, scale), out_shape=(grad,...  37.5 us
    pallas_call x1, Pallas kernels, gather_weights(): pl.pallas_call(gather_kernel, out_shape=(full, full, cut, cut, jax.ShapeD...  30.5 us
    pallas_call x1, Pallas kernels, local_layer(): pl.pallas_call(layer_kernel, out_shape=(result, result, kept, kept), in_s...  13.9 us

profile of v5, /device:TPU:1, one launch (start us, length us, event | category | flops | bytes accessed | tf_op | source)
XLA Modules:
  0.0 84.0 jit_solution(7580638779583153722)
XLA Ops:
  0.6 0.0 copy-start
  0.6 0.0 copy-start.1
  0.7 30.5 %gather_weights.1 = (bf16[32,4,128,128]{3,2,1,0:T(8,128)(2,1)S(1)}, bf16[32,4,128,128]{3,2,1,0:T(8,128)(2,1)S(1)}, bf16[48,256,128]{2,1,0:T(8,128)(2,1)S(1)}, bf...) custom-call(s32[1,128]{1,0:T(1,128)} %bitcast.6, s32[1,128]{1,0:T(1,128)} %bitcast.7, s32[32]{0:T(128)} %counts_hbm.1, ...), custom_call_target="tpu_custom_call" | custom-call | tf_op jit(solution)/shard_map/gather_weights/pallas_call | solution.py:253
  31.2 0.0 copy-done
  31.2 0.0 copy-done.1
  31.2 13.9 %local_layer.1 = (bf16[256,6144]{1,0:T(8,128)(2,1)}, bf16[256,6144]{1,0:T(8,128)(2,1)}, bf16[130,256,128]{2,1,0:T(8,128)(2,1)S(1)}, bf16[130,256,128]{2,1,0:T(8,128)(2,1)S(1)}) custom-call(s32[128]{0:T(128)S(1)} %copy-done, s32[128]{0:T(128)S(1)} %copy-done.1, s32[8,128]{1,0:T(8,128)S(1)} %get-tuple-element.15.tab, ...), custom_call_target="tpu_custom_call" | custom-call | tf_op jit(solution)/shard_map/local_layer/pallas_call | solution.py:375
  45.0 37.5 %scatter_grads.1 = (f32[4,128,128]{2,1,0:T(8,128)S(1)}, f32[4,128,128]{2,1,0:T(8,128)S(1)}) custom-call(s32[128]{0:T(128)S(1)} %copy-done, s32[8,128]{1,0:T(8,128)S(1)} %get-tuple-element.15.tab, bf16[48,256,128]{2,1,0:T(8,128)(2,1)S(1)} %get-tuple-element.16.x, bf16[48,256,128]{2,1,0:T(8,128)(2,1)S(1)} %get-tuple-element.17.dy, ...), custom_call_target="tpu_custom_call" | custom-call | tf_op jit(solution)/shard_map/scatter_grads/pallas_call | solution.py:570
  82.6 0.7 copy.13
  83.3 0.7 copy.14
Async XLA Ops:
  0.6 30.5 %copy-start = (s32[128]{0:T(128)S(1)}, s32[128]{0:T(128)}, u32[]{:S(2)}) copy-start(s32[128]{0:T(128)} %rows.3) | copy-start | bytes 1540
  0.6 30.5 %copy-start.1 = (s32[128]{0:T(128)S(1)}, s32[128]{0:T(128)}, u32[]{:S(2)}) copy-start(s32[128]{0:T(128)} %cols.1) | copy-start | bytes 1540

commit v6 on v5

--- a/solution.py
+++ b/solution.py
@@ -515,7 +515,8 @@
     )
     lax.fori_loop(0, 4, turns(lambda i: give(i, 2)), 0)
     lax.fori_loop(0, 4, turns(far, make_give(3), make_give(1)), 0)
-    lax.fori_loop(0, 4, turns(near, make_give(0)), 0)
+    lax.fori_loop(0, 4, turns(near), 0)
+    lax.fori_loop(0, 4, turns(make_give(0)), 0)
     lax.fori_loop(0, 4, turns(stay), 0)
     pass_on(0, 2, 0, mid2, first_p)
     pass_on(1, 2, 1, mid2, first_m)

time: 84.1 us -> 83.3 us (level)
  no operation moved by 1% of the time
where the time goes in v6:
time: 83.3 us; the launch traced here: 83.4 us
  Pallas kernels  81.3 us (98%)
  local copies, waits for them, and re-layouts  1.42 us (2%)
    pallas_call x1, Pallas kernels, scatter_grads(): pl.pallas_call(functools.partial(scatter_kernel, scale), out_shape=(grad,...  37.5 us
    pallas_call x1, Pallas kernels, gather_weights(): pl.pallas_call(gather_kernel, out_shape=(full, full, cut, cut, jax.ShapeD...  30.5 us
    pallas_call x1, Pallas kernels, local_layer(): pl.pallas_call(layer_kernel, out_shape=(result, result, kept, kept), in_s...  13.3 us

profile of v6, /device:TPU:1, one launch (start us, length us, event | category | flops | bytes accessed | tf_op | source)
XLA Modules:
  0.0 83.4 jit_solution(2544572099267725980)
XLA Ops:
  0.6 0.0 copy-start
  0.6 0.0 copy-start.1
  0.7 30.5 %gather_weights.1 = (bf16[32,4,128,128]{3,2,1,0:T(8,128)(2,1)S(1)}, bf16[32,4,128,128]{3,2,1,0:T(8,128)(2,1)S(1)}, bf16[48,256,128]{2,1,0:T(8,128)(2,1)S(1)}, bf...) custom-call(s32[1,128]{1,0:T(1,128)} %bitcast.6, s32[1,128]{1,0:T(1,128)} %bitcast.7, s32[32]{0:T(128)} %counts_hbm.1, ...), custom_call_target="tpu_custom_call" | custom-call | tf_op jit(solution)/shard_map/gather_weights/pallas_call | solution.py:253
  31.2 0.0 copy-done
  31.2 0.0 copy-done.1
  31.2 13.3 %local_layer.1 = (bf16[256,6144]{1,0:T(8,128)(2,1)}, bf16[256,6144]{1,0:T(8,128)(2,1)}, bf16[130,256,128]{2,1,0:T(8,128)(2,1)S(1)}, bf16[130,256,128]{2,1,0:T(8,128)(2,1)S(1)}) custom-call(s32[128]{0:T(128)S(1)} %copy-done, s32[128]{0:T(128)S(1)} %copy-done.1, s32[8,128]{1,0:T(8,128)S(1)} %get-tuple-element.15.tab, ...), custom_call_target="tpu_custom_call" | custom-call | tf_op jit(solution)/shard_map/local_layer/pallas_call | solution.py:375
  44.5 37.5 %scatter_grads.1 = (f32[4,128,128]{2,1,0:T(8,128)S(1)}, f32[4,128,128]{2,1,0:T(8,128)S(1)}) custom-call(s32[128]{0:T(128)S(1)} %copy-done, s32[8,128]{1,0:T(8,128)S(1)} %get-tuple-element.15.tab, bf16[48,256,128]{2,1,0:T(8,128)(2,1)S(1)} %get-tuple-element.16.x, bf16[48,256,128]{2,1,0:T(8,128)(2,1)S(1)} %get-tuple-element.17.dy, ...), custom_call_target="tpu_custom_call" | custom-call | tf_op jit(solution)/shard_map/scatter_grads/pallas_call | solution.py:571
  82.0 0.7 copy.13
  82.7 0.7 copy.14
Async XLA Ops:
  0.6 30.5 %copy-start = (s32[128]{0:T(128)S(1)}, s32[128]{0:T(128)}, u32[]{:S(2)}) copy-start(s32[128]{0:T(128)} %rows.3) | copy-start | bytes 1540
  0.6 30.5 %copy-start.1 = (s32[128]{0:T(128)S(1)}, s32[128]{0:T(128)}, u32[]{:S(2)}) copy-start(s32[128]{0:T(128)} %cols.1) | copy-start | bytes 1540
